TPU v7x, 32 devices: a whole 2x2x4 slice. The times are simulated.
32 devices in a mesh: wave: 8 (over z, core), lev: 4 (over y, x).
Axes of the slice: x: 2, y: 2, z: 4, core: 2. Of those that a mesh axis runs over, the one named last changes fastest.
Arguments:
- spectrum: bfloat16 [4, 4, 2, 1280, 1280], P(None, 'lev', None, 'wave'), may hold values from -6 to 6
- legendre: bfloat16 [1280, 8, 1280], P('wave'), may hold values from -0.15625 to 0.15625
- order_of_slot: int32 [1280], replicated, may hold values from 0 to 1279, each once
- reduced_length: int32 [8], replicated, may hold values from 20 to 5136, as said below
- gauss_weight: float32 [8], P('wave'), may hold values from 2 to 6
- depart_row: int32 [2, 4, 4, 8, 5632], P(None, 'lev', None, 'wave'), may hold values from -1 to 1, as said below
- depart_col: int32 [2, 4, 4, 8, 5632], P(None, 'lev', None, 'wave'), may hold values from 0 to 5135, as said below
- depart_weight: float32 [2, 4, 4, 8, 5632], P(None, 'lev', None, 'wave'), may hold values from 0.05 to 0.5
Outputs:
- spectrum_out: bfloat16 [4, 4, 2, 1280, 1280], P(None, 'lev', None, 'wave')
Inputs may be any that keep to these rules, and one draw needn't show every extreme that they name: `reduced_length`: each latitude j has 20 + 4 i points for a cycle i with j * 160 <= i < (j + 1) * 160; the last latitude has 5136. `depart_row`: offset of the departure latitude from the arrival latitude; a departure latitude outside the window reads zeros. `depart_col`: below the reduced length of the departure latitude (of the nearest window latitude where it lies outside the window). `order_of_slot`: A permutation of the zonal orders.
All inputs are finite; a program needn't handle non-finite values.
Results may differ from a plain program's by a relative error of at most 0.02.
Values may be sent and summed in bfloat16 or wider, within the bound.
A program may use at most 128 MiB of HBM per device.

v0:
```python
import math

import jax
import jax.numpy as jnp
from jax import lax
from jax.sharding import PartitionSpec as P

BLOCK = 512


full_turn = 2.0 * math.pi


def extended_2(block, sides, width):
    for axis, dim in sides:
        count = lax.axis_size(axis)
        forward = [(i, i + 1) for i in range(count - 1)]
        backward = [(target, source) for source, target in forward]
        low = lax.ppermute(
            lax.slice_in_dim(block, block.shape[dim] - width, None, axis=dim), axis, forward
        )
        high = lax.ppermute(lax.slice_in_dim(block, 0, width, axis=dim), axis, backward)
        block = jnp.concatenate([low, block, high], axis=dim)
    return block


def base_table(length, orders, order_limit, block_width):
    offsets = jnp.arange(block_width, dtype=jnp.int32)
    phases = orders[:, None] * offsets[None, :] % length
    angles = phases.astype(jnp.float32) * (jnp.float32(full_turn) / length.astype(jnp.float32))
    active = (orders < order_limit)[:, None]
    cosine = jnp.where(active, jnp.cos(angles), 0.0)
    sine_part = jnp.where(active, -jnp.sin(angles), 0.0)
    return jnp.concatenate([cosine, sine_part], axis=0).astype(jnp.bfloat16)


def block_phases(length, orders, grid_width, block_width):
    starts = jnp.arange(grid_width // block_width, dtype=jnp.int32) * block_width
    phases = starts[:, None] * orders[None, :] % length
    angles = phases.astype(jnp.float32) * (jnp.float32(full_turn) / length.astype(jnp.float32))
    return (jnp.cos(angles), jnp.sin(angles))


def synthesize(coeffs, length, order_limit, fourier_table, cos_phase, sin_phase):
    field_count = coeffs.shape[0]
    blocks = cos_phase.shape[0]
    block_width = fourier_table.shape[1]
    real_part = coeffs[:, 0, :].astype(jnp.float32)[:, None, :]
    imag_part = coeffs[:, 1, :].astype(jnp.float32)[:, None, :]
    rot_real = real_part * cos_phase[None] - imag_part * sin_phase[None]
    rot_imag = real_part * sin_phase[None] + imag_part * cos_phase[None]
    rotated = jnp.stack([rot_real, rot_imag], axis=2).astype(jnp.bfloat16)
    rotated = rotated.reshape(field_count * blocks, -1)
    result = jnp.dot(rotated, fourier_table, preferred_element_type=jnp.float32)
    result = result.reshape(field_count, blocks * block_width)
    points = jnp.arange(blocks * block_width, dtype=jnp.int32)
    factor = 1.0 / jnp.sqrt(order_limit.astype(jnp.float32))
    return jnp.where(points[None, :] < length, result * factor, 0.0)


def analyse(newgrid, fourier_table, cos_phase, sin_phase):
    field_count = newgrid.shape[0]
    blocks = cos_phase.shape[0]
    block_width = fourier_table.shape[1]
    partial_value = lax.dot_general(
        newgrid.reshape(field_count * blocks, block_width),
        fourier_table,
        (((1,), (1,)), ((), ())),
        preferred_element_type=jnp.float32,
    )
    partial_value = partial_value.reshape(field_count, blocks, 2, -1)
    part_real = partial_value[:, :, 0, :]
    part_imag = partial_value[:, :, 1, :]
    real_sum = jnp.sum(part_real * cos_phase[None] + part_imag * sin_phase[None], axis=1)
    imag_sum = jnp.sum(part_imag * cos_phase[None] - part_real * sin_phase[None], axis=1)
    return jnp.stack([real_sum, imag_sum], axis=1)


def per_device(
    spectrum,
    legendre,
    order_of_slot,
    reduced_length,
    gauss_weight,
    depart_row,
    depart_col,
    depart_weight,
):
    own_index = lax.axis_index("wave")
    slot_count = legendre.shape[0]
    orders_total = order_of_slot.shape[0]
    variables = spectrum.shape[0]
    level_count = spectrum.shape[1]
    field_count = variables * level_count
    grid_width = depart_row.shape[-1]
    stencil = depart_row.shape[2]
    own_orders = lax.dynamic_slice_in_dim(order_of_slot, own_index * slot_count, slot_count)
    degrees = jnp.arange(legendre.shape[2], dtype=jnp.int32)
    masked = jnp.where(
        degrees[None, None, :] >= own_orders[:, None, None], legendre, jnp.zeros((), jnp.bfloat16)
    )
    length = lax.dynamic_index_in_dim(reduced_length, own_index, keepdims=False)
    order_limit = jnp.minimum(orders_total, (length - 1) // 2)
    fourier_table = base_table(length, order_of_slot, order_limit, BLOCK)
    cos_phase, sin_phase = block_phases(length, order_of_slot, grid_width, BLOCK)
    own_info = (length, order_limit, fourier_table, cos_phase, sin_phase)
    weight = gauss_weight[0]
    points = jnp.arange(grid_width, dtype=jnp.int32)
    level_base = (jnp.arange(level_count, dtype=jnp.int32) * (3 * grid_width))[:, None, None]
    spectral_state = spectrum
    for step_index in range(depart_row.shape[0]):
        fourier = jnp.einsum(
            "vlcsn,sjn->jvlcs", spectral_state, masked, preferred_element_type=jnp.float32
        ).astype(jnp.bfloat16)
        gathered = lax.all_to_all(fourier, "wave", split_axis=0, concat_axis=4, tiled=True)
        own_grid = synthesize(
            gathered.reshape(field_count, 2, orders_total),
            own_info[0],
            own_info[1],
            own_info[2],
            own_info[3],
            own_info[4],
        )
        extended = extended_2(
            own_grid.reshape(variables, level_count, 1, grid_width).astype(jnp.bfloat16),
            (("wave", 2),),
            1,
        ).astype(jnp.float32)
        flat_rows = extended.reshape(variables, level_count * 3 * grid_width)
        row_offsets = depart_row[step_index][:, :, 0, :]
        columns = depart_col[step_index][:, :, 0, :]
        weights = depart_weight[step_index][:, :, 0, :]
        flat_index = (level_base + (row_offsets + 1) * grid_width + columns).reshape(-1)
        values = jnp.take(flat_rows, flat_index, axis=1)
        values = values.reshape(variables, level_count, stencil, grid_width)
        interp = jnp.sum(values * weights[None], axis=2)
        tendency = interp + 0.5 * jnp.roll(interp, -1, axis=0) * jnp.tanh(
            jnp.roll(interp, -2, axis=0)
        )
        newgrid = jnp.where(points < own_info[0], tendency, 0.0).astype(jnp.bfloat16)
        analysed = analyse(
            newgrid.reshape(field_count, grid_width), own_info[2], own_info[3], own_info[4]
        )
        coeffs = (analysed * (weight * jnp.sqrt(2.0 / own_info[0].astype(jnp.float32)))).astype(
            jnp.bfloat16
        )
        coeffs = coeffs.reshape(1, variables, level_count, 2, orders_total)
        returned = lax.all_to_all(coeffs, "wave", split_axis=4, concat_axis=0, tiled=True)
        spectral_state = jnp.einsum(
            "jvlcs,sjn->vlcsn", returned, masked, preferred_element_type=jnp.float32
        ).astype(jnp.bfloat16)
    return spectral_state


def solution(mesh):
    placed = (
        P(None, "lev", None, "wave", None),
        P("wave", None, None),
        P(),
        P(),
        P("wave"),
        P(None, "lev", None, "wave", None),
        P(None, "lev", None, "wave", None),
        P(None, "lev", None, "wave", None),
    )
    return jax.shard_map(
        per_device,
        mesh=mesh,
        in_specs=placed,
        out_specs=P(None, "lev", None, "wave", None),
        check_vma=False,
    )
```

profile of v0, /device:TPU:0, one launch (start us, length us, event | category | flops | bytes accessed | tf_op | source)
XLA Modules:
  0.0 356.6 jit_solution(9272613454068507887)
XLA Ops:
  0.0 0.9 dynamic_slice.7
  1.1 0.8 copy-done
  2.6 5.7 %fusion.31 = bf16[8,4,1,2,160]{0,1,3,4,2:T(4,128)(2,1)} fusion(bf16[4,2,160,1280]{3,2,1,0:T(8,128)(2,1)S(1)} %bitcast.183, bf16[160,8,1280]{2,1,0:T(8,128)(2,1)} %param.11, pred[160,1280]{1,0:T(8,128)(4,1)S(1)} %iota_compare_fusion), kind=kOutput, calls=%fused_computation.38 | convolution fusion | flops 27863040 | bytes 6778880 | tf_op jit(solution)/shard_map/vlcsn,sjn->jvlcs/dot_general | solution.py:112
  8.3 2.0 copy.155
  10.3 6.4 %all-to-all-start = ((bf16[8,4,1,2,160]{4,1,3,2,0:T(4,128)(2,1)}), bf16[8,4,1,2,160]{4,1,3,2,0:T(4,128)(2,1)S(1)}, u32[]{:S(2)}, u32[]{:S(2)}) async-start(bf16[8,4,1,2,160]{4,1,3,2,0:T(4,128)(2,1)} %copy.155), calls=%async_computation | async-start | bytes 65536 | tf_op jit(solution)/shard_map/all_to_all | solution.py:115
  19.2 1.3 slice_add_fusion
  21.2 1.2 fusion.57
  22.4 36.4 %select_convert_fusion.1 = (bf16[1280,512]{1,0:T(8,128)(2,1)S(1)}, bf16[1280,512]{1,0:T(8,128)(2,1)S(1)}) fusion(f32[]{:T(128)S(6)} %div.18, s32[]{:T(128)S(6)} %select_n.124, s32[1280]{0:T(1024)S(1)} %copy-done.13, pred[1280]{0:T(1024)(128)(4,1)S(1)} %broadcast_compare_fusion, pred[]{:T(512)S(6)} %lt.62), kind=kLoop, calls=%fused_computation.27 | loop fusion | flops 9830400 | bytes 2627849 | tf_op jit(solution)/shard_map/convert.8
  58.9 0.8 copy_bitcast_fusion
  62.5 2.4 collective-permute-start
  64.9 1.5 collective-permute-start.1
  66.4 1.7 pad_maximum_fusion
  69.3 4.9 %copy.157 = f32[4,1,3,5632]{0,3,2,1:T(8,128)} copy(f32[4,1,3,5632]{3,0,2,1:T(4,128)S(1)} %maximum_convert_fusion) | data formatting | bytes 540672 | tf_op jit(solution)/shard_map/convert_element_type | solution.py:128
  74.2 78.1 %gather_fusion = f32[22528,4]{1,0:T(8,128)} fusion(f32[4,16896]{0,1:T(8,128)} %bitcast.186, s32[22528]{0:T(1024)S(1)} %fusion.60), kind=kCustom, calls=%fused_computation.clone | custom fusion | bytes 811008 | tf_op jit(solution)/shard_map/jit(_take)/gather | solution.py:134
  152.3 12.9 %broadcast_select_fusion.1 = f32[22528,4]{1,0:T(8,128)S(1)} fusion(f32[22528,4]{1,0:T(8,128)} %gather_fusion, pred[22528]{0:T(1024)(128)(4,1)S(1)} %compare_and_fusion.1), kind=kLoop, calls=%fused_computation.5 | loop fusion | flops 90112 | bytes 743424 | tf_op jit(solution)/shard_map/jit(_take)/select_n | solution.py:134
  165.2 3.9 %multiply_reduce_fusion.1 = f32[4,5632]{0,1:T(8,128)S(1)} fusion(f32[4,1,4,5632]{0,3,2,1:T(8,128)S(1)} %bitcast.185, f32[4,5632]{1,0:T(4,128)S(1)} %copy-done.11), kind=kLoop, calls=%fused_computation.3 | loop fusion | flops 157696 | bytes 540672 | tf_op jit(solution)/shard_map/reduce_sum | solution.py:136
  169.1 2.4 slice_bitcast_fusion.1
  171.5 0.8 copy.158
  172.3 0.8 slice_reduce_fusion.1
  173.1 2.8 copy.159
  176.2 0.9 fusion.62
  177.9 2.1 copy.164
  180.0 2.7 reshape.894
  182.7 12.4 %all_to_all.60 = bf16[8,2,640]{2,1,0:T(2,128)(2,1)} all-to-all(bf16[8,2,640]{2,1,0:T(2,128)(2,1)} %reshape.894), channel_id=1, replica_groups=mesh['wave'=8,'lev'=4] {'wave'}, dimensions={0} | all-to-all | bytes 40960 | tf_op jit(solution)/shard_map/all_to_all | solution.py:148
  195.1 2.9 reshape.895
  198.0 4.0 %copy.166 = bf16[1,4,1,2,8,160]{4,1,3,5,2,0:T(4,128)(2,1)} copy(bf16[1,4,1,2,8,160]{1,3,5,4,2,0:T(2,128)(2,1)} %bitcast.191) | data formatting | bytes 40960 | tf_op jit(solution)/shard_map/all_to_all | solution.py:148
  202.0 6.1 %fusion.36 = bf16[8,4,1,2,160]{0,1,3,4,2:T(4,128)(2,1)} fusion(bf16[160,8,1280]{2,1,0:T(8,128)(2,1)S(1)} %copy-done.8, pred[160,1280]{1,0:T(8,128)(4,1)} %copy-done.9, bf16[1,4,1,2,8,160]{4,1,3,5,2,0:T(4,128)(2,1)} %copy.166), kind=kOutput, calls=%fused_computation.39 | convolution fusion | flops 57354240 | bytes 3522560 | tf_op jit(solution)/shard_map/vlcsn,sjn->jvlcs/dot_general | solution.py:112
  208.1 2.1 copy.167
  210.2 3.5 all-to-all-start.2
  213.8 5.4 %all-to-all-done.2 = bf16[8,4,1,2,160]{4,1,3,2,0:T(4,128)(2,1)S(1)} async-done(((bf16[8,4,1,2,160]{4,1,3,2,0:T(4,128)(2,1)}), bf16[8,4,1,2,160]{4,1,3,2,0:T(4,128)(2,1)S(1)}, u32[]{:S(2)}, u32[]{:S(2)}) %all-to-all-start.2) | async-done | bytes 20512 | tf_op jit(solution)/shard_map/all_to_all | solution.py:115
  221.3 1.6 collective-permute-start.2
  222.9 1.3 collective-permute-start.3
  224.3 2.3 collective-permute-done.3
  226.7 4.9 %copy.169 = f32[4,1,3,5632]{0,3,2,1:T(8,128)} copy(f32[4,1,3,5632]{3,0,2,1:T(4,128)S(1)} %maximum_convert_fusion.1) | data formatting | bytes 540672 | tf_op jit(solution)/shard_map/convert_element_type | solution.py:128
  231.6 78.1 %gather_fusion.1 = f32[22528,4]{1,0:T(8,128)} fusion(f32[4,16896]{0,1:T(8,128)} %bitcast.187, s32[22528]{0:T(1024)S(1)} %fusion.61), kind=kCustom, calls=%fused_computation.1.clone | custom fusion | bytes 811008 | tf_op jit(solution)/shard_map/jit(_take)/gather | solution.py:134
  309.7 12.9 %broadcast_select_fusion = f32[22528,4]{1,0:T(8,128)S(1)} fusion(f32[22528,4]{1,0:T(8,128)} %gather_fusion.1, pred[22528]{0:T(1024)(128)(4,1)S(1)} %compare_and_fusion), kind=kLoop, calls=%fused_computation.4 | loop fusion | flops 90112 | bytes 743424 | tf_op jit(solution)/shard_map/jit(_take)/select_n | solution.py:134
  322.6 3.9 %multiply_reduce_fusion = f32[4,5632]{0,1:T(8,128)S(1)} fusion(f32[4,1,4,5632]{0,3,2,1:T(8,128)S(1)} %bitcast.184, f32[4,5632]{1,0:T(4,128)S(1)} %copy-done.10), kind=kLoop, calls=%fused_computation.2 | loop fusion | flops 157696 | bytes 540672 | tf_op jit(solution)/shard_map/reduce_sum | solution.py:136
  326.5 2.4 slice_bitcast_fusion
  328.9 0.8 copy.170
  329.7 0.8 slice_reduce_fusion
  330.6 2.8 copy.171
  333.6 0.9 fusion.71
  335.3 1.0 reshape.896
  336.3 9.6 %all_to_all.61 = bf16[8,2,640]{2,1,0:T(2,128)(2,1)S(1)} all-to-all(bf16[8,2,640]{2,1,0:T(2,128)(2,1)S(1)} %reshape.896), channel_id=1, replica_groups=mesh['wave'=8,'lev'=4] {'wave'}, dimensions={0} | all-to-all | bytes 40960 | tf_op jit(solution)/shard_map/all_to_all | solution.py:148
  345.9 1.3 reshape.897
  347.2 3.0 copy.179
  350.2 4.0 %fusion.1 = bf16[4,1,2,160,1280]{4,0,2,3,1:T(4,128)(2,1)S(1)} fusion(bf16[160,8,1280]{2,1,0:T(8,128)(2,1)} %param.11, pred[160,1280]{1,0:T(8,128)(4,1)} %copy-done.9, bf16[1,4,1,2,8,160]{4,1,3,5,2,0:T(4,128)(2,1)} %copy.179), kind=kOutput, calls=%fused_computation.10 | convolution fusion | flops 29491200 | bytes 6778880 | tf_op jit(solution)/shard_map/jvlcs,sjn->vlcsn/dot_general | solution.py:149
  354.3 2.3 copy.180
  (81 shorter events, 8.8 us)
Async XLA Ops:
  0.0 1.9 copy-start
  1.9 0.7 copy-start.9
  2.6 14.0 %copy-start.14 = (s32[8]{0:T(128)S(1)}, s32[8]{0:T(128)}, u32[]{:S(2)}) copy-start(s32[8]{0:T(128)} %param.13) | copy-start | bytes 100
  2.6 18.5 %copy-start.13 = (s32[1280]{0:T(1024)S(1)}, s32[1280]{0:T(1024)}, u32[]{:S(2)}) copy-start(s32[1280]{0:T(1024)} %param.12) | copy-start | bytes 15364
  8.3 50.6 %copy-start.12 = (f32[2,1,4,1,5632]{4,3,2,1,0:T(1,128)S(1)}, f32[2,1,4,1,5632]{4,3,2,1,0:T(1,128)}, u32[]{:S(2)}) copy-start(f32[2,1,4,1,5632]{4,3,2,1,0:T(1,128)} %param.17) | copy-start | bytes 540676
  10.3 50.2 %all-to-all-start = ((bf16[8,4,1,2,160]{4,1,3,2,0:T(4,128)(2,1)}), bf16[8,4,1,2,160]{4,1,3,2,0:T(4,128)(2,1)S(1)}, u32[]{:S(2)}, u32[]{:S(2)}) async-start(bf16[8,4,1,2,160]{4,1,3,2,0:T(4,128)(2,1)} %copy.155), calls=%async_computation | async-start | bytes 65536 | tf_op jit(solution)/shard_map/all_to_all | solution.py:115
  58.9 7.5 %copy-start.4 = (bf16[1280,512]{1,0:T(8,128)(2,1)}, bf16[1280,512]{1,0:T(8,128)(2,1)S(1)}, u32[]{:S(2)}) copy-start(bf16[1280,512]{1,0:T(8,128)(2,1)S(1)} %get-tuple-element.26) | copy-start | bytes 3932164
  58.9 7.5 %copy-start.6 = (bf16[1280,512]{1,0:T(8,128)(2,1)}, bf16[1280,512]{1,0:T(8,128)(2,1)S(1)}, u32[]{:S(2)}) copy-start(bf16[1280,512]{1,0:T(8,128)(2,1)S(1)} %get-tuple-element.27) | copy-start | bytes 3932164
  62.5 6.3 %collective-permute-start = (bf16[4,1,1,5632]{3,0,2,1:T(4,128)(2,1)S(1)}, bf16[4,1,1,5632]{3,0,2,1:T(4,128)(2,1)S(1)}, u32[]{:S(2)}, u32[]{:S(2)}) collective-permute-start(bf16[4,1,1,5632]{3,0,2,1:T(4,128)(2,1)S(1)} %select_convert_fusion.3), channel_id=1, source_target_pairs={{0,4},{4,8},{8,12},{12,16},{16,20},{20,24},{24,28},{1,5},{5,9},{9,... | collective-permute-start | bytes 135176 | tf_op jit(solution)/shard_map/ppermute | solution.py:19
  64.9 4.3 %collective-permute-start.1 = (bf16[4,1,1,5632]{3,0,2,1:T(4,128)(2,1)S(1)}, bf16[4,1,1,5632]{3,0,2,1:T(4,128)(2,1)S(1)}, u32[]{:S(2)}, u32[]{:S(2)}) collective-permute-start(bf16[4,1,1,5632]{3,0,2,1:T(4,128)(2,1)S(1)} %select_convert_fusion.3), channel_id=1, source_target_pairs={{4,0},{8,4},{12,8},{16,12},{20,16},{24,20},{28,24},{5,1},{9,5},{13... | collective-permute-start | bytes 135176 | tf_op jit(solution)/shard_map/ppermute | solution.py:22
  152.3 12.9 %copy-start.11 = (f32[4,5632]{1,0:T(4,128)S(1)}, f32[4,5632]{1,0:T(4,128)}, u32[]{:S(2)}) copy-start(f32[4,5632]{1,0:T(4,128)} %get-tuple-element.33) | copy-start | bytes 270340
  173.1 3.1 copy-start.2
  177.1 24.9 %copy-start.8 = (bf16[160,8,1280]{2,1,0:T(8,128)(2,1)S(1)}, bf16[160,8,1280]{2,1,0:T(8,128)(2,1)}, u32[]{:S(2)}) copy-start(bf16[160,8,1280]{2,1,0:T(8,128)(2,1)} %param.11) | copy-start | bytes 9830404
  208.1 12.5 %copy-start.5 = (bf16[1280,512]{1,0:T(8,128)(2,1)S(1)}, bf16[1280,512]{1,0:T(8,128)(2,1)}, u32[]{:S(2)}) copy-start(bf16[1280,512]{1,0:T(8,128)(2,1)} %copy-done.4) | copy-start | bytes 3932164
  208.1 12.5 %copy-start.7 = (bf16[1280,512]{1,0:T(8,128)(2,1)S(1)}, bf16[1280,512]{1,0:T(8,128)(2,1)}, u32[]{:S(2)}) copy-start(bf16[1280,512]{1,0:T(8,128)(2,1)} %copy-done.6) | copy-start | bytes 3932164
  210.2 9.0 %all-to-all-start.2 = ((bf16[8,4,1,2,160]{4,1,3,2,0:T(4,128)(2,1)}), bf16[8,4,1,2,160]{4,1,3,2,0:T(4,128)(2,1)S(1)}, u32[]{:S(2)}, u32[]{:S(2)}) async-start(bf16[8,4,1,2,160]{4,1,3,2,0:T(4,128)(2,1)} %copy.167), calls=%async_computation.2 | async-start | bytes 65536 | tf_op jit(solution)/shard_map/all_to_all | solution.py:115
  221.3 3.0 collective-permute-start.2
  222.9 3.7 %collective-permute-start.3 = (bf16[4,1,1,5632]{3,0,2,1:T(4,128)(2,1)S(1)}, bf16[4,1,1,5632]{3,0,2,1:T(4,128)(2,1)S(1)}, u32[]{:S(2)}, u32[]{:S(2)}) collective-permute-start(bf16[4,1,1,5632]{3,0,2,1:T(4,128)(2,1)S(1)} %select_convert_fusion.2), channel_id=1, source_target_pairs={{4,0},{8,4},{12,8},{16,12},{20,16},{24,20},{28,24},{5,1},{9,5},{13... | collective-permute-start | bytes 135176 | tf_op jit(solution)/shard_map/ppermute | solution.py:22
  309.7 12.9 %copy-start.10 = (f32[4,5632]{1,0:T(4,128)S(1)}, f32[4,5632]{1,0:T(4,128)}, u32[]{:S(2)}) copy-start(f32[4,5632]{1,0:T(4,128)} %get-tuple-element.32) | copy-start | bytes 270340
  330.6 3.1 copy-start.3
  350.2 6.4 %copy-start.1 = (bf16[4,1,2,160,1280]{4,3,2,1,0:T(8,128)(2,1)S(1)}, bf16[4,1,2,160,1280]{4,3,2,1,0:T(8,128)(2,1)}, u32[]{:S(2)}) copy-start(bf16[4,1,2,160,1280]{4,3,2,1,0:T(8,128)(2,1)} %param.10) | copy-start | bytes 9830404
where the time goes:
time: 357 us
  local copies, waits for them, and re-layouts  209 us (59%)
  other arithmetic  78.6 us (22%)
  blocking collectives  22 us (6%)
  matrix products  18.7 us (5%)
  starting transfers between devices  16.7 us (5%)
  waiting for transfers between devices  8.07 us (2%)
  between operations  3.92 us (1%)
    gather x2, local copies, waits for them, and re-layouts, per_device(): values = jnp.take(flat_rows, flat_index, axis=1)  156 us
    another operation x3, other arithmetic  37.4 us
    select_n x2, other arithmetic, per_device(): values = jnp.take(flat_rows, flat_index, axis=1)  25.7 us
    all_to_all x2, blocking collectives, per_device(): lax.all_to_all(coeffs, 'wave', split_axis=4, concat_axis=0, tiled=True)  22 us
    dot_general x2, matrix products, per_device(): jnp.einsum('vlcsn,sjn->jvlcs', spectral_state, masked, preferred_element_...  11.8 us
    unnamed x42, local copies, waits for them, and re-layouts  10.8 us
    concatenate x6, local copies, waits for them, and re-layouts, per_device(): jnp.roll(interp, -1, axis=0)  10.4 us
    all_to_all x2, starting transfers between devices, per_device(): lax.all_to_all(fourier, 'wave', split_axis=0, concat_axis=4, tiled=True)  9.9 us
  transfers between devices with their start and end apart: 6, of which 3 were waited for; matrix products, arithmetic and copies ran while one was open for 12% of the time, Pallas kernels for 0%

commit v1 on v0

v1 whole, which is shorter than its diff:
```python
import functools
import math

import jax
import jax.numpy as jnp
from jax import lax
from jax.experimental import pallas as pl
from jax.experimental.pallas import tpu as pltpu
from jax.sharding import PartitionSpec as P

BLOCK = 512
RADIX = 8
FULL_TURN = 2.0 * math.pi
F32 = jnp.float32
BF16 = jnp.bfloat16

VMEM_SPEC = pl.BlockSpec(memory_space=pltpu.VMEM)
SMEM_SPEC = pl.BlockSpec(memory_space=pltpu.SMEM)


def padded_blocks(grid_width):
    return -(-(grid_width // BLOCK) // 16) * 16


def phase_rows(length, orders, blocks):
    digits = jnp.arange(RADIX, dtype=jnp.int32)
    steps = [digits, digits * RADIX, digits * RADIX * RADIX]
    steps.append(jnp.arange(blocks, dtype=jnp.int32) * BLOCK)
    steps = jnp.concatenate(steps)
    phases = steps[:, None] * orders[None, :] % length
    angles = phases.astype(F32) * (jnp.float32(FULL_TURN) / length.astype(F32))
    return jnp.cos(angles), jnp.sin(angles)


def table_kernel(cos_ref, sin_ref, active_ref, fc_ref, fs_ref, ca_ref, sa_ref):
    active = active_ref[...]
    cos_low = cos_ref[0:RADIX, :] * active
    sin_low = sin_ref[0:RADIX, :] * active
    cos_mid = cos_ref[RADIX : 2 * RADIX, :]
    sin_mid = sin_ref[RADIX : 2 * RADIX, :]
    for a in range(RADIX):
        c = cos_ref[2 * RADIX + a : 2 * RADIX + a + 1, :]
        s = sin_ref[2 * RADIX + a : 2 * RADIX + a + 1, :]
        ca_ref[a * RADIX : (a + 1) * RADIX, :] = c * cos_mid - s * sin_mid
        sa_ref[a * RADIX : (a + 1) * RADIX, :] = s * cos_mid + c * sin_mid

    def body(i, carry):
        cos_parts, sin_parts = [], []
        for k in range(2):
            c = ca_ref[pl.ds(2 * i + k, 1), :]
            s = sa_ref[pl.ds(2 * i + k, 1), :]
            cos_parts.append(c * cos_low - s * sin_low)
            sin_parts.append(-(s * cos_low + c * sin_low))
        rows = pl.ds(pl.multiple_of(i * 2 * RADIX, 2 * RADIX), 2 * RADIX)
        fc_ref[rows, :] = jnp.concatenate(cos_parts, axis=0).astype(BF16)
        fs_ref[rows, :] = jnp.concatenate(sin_parts, axis=0).astype(BF16)
        return carry

    lax.fori_loop(0, RADIX * RADIX // 2, body, 0)


def synthesize(coeffs, cos_block, sin_block, fc_ref, fs_ref, length, scale):
    fields = coeffs.shape[0] // 2
    blocks = cos_block.shape[0]
    reals, imags = [], []
    for v in range(fields):
        real = coeffs[2 * v : 2 * v + 1]
        imag = coeffs[2 * v + 1 : 2 * v + 2]
        reals.append((real * cos_block - imag * sin_block).astype(BF16))
        imags.append((real * sin_block + imag * cos_block).astype(BF16))
    dims = (((1,), (1,)), ((), ()))
    out = lax.dot_general(
        jnp.concatenate(reals, axis=0), fc_ref[...], dims, preferred_element_type=F32
    ) + lax.dot_general(
        jnp.concatenate(imags, axis=0), fs_ref[...], dims, preferred_element_type=F32
    )
    row = lax.broadcasted_iota(jnp.int32, out.shape, 0) % blocks
    point = row * BLOCK + lax.broadcasted_iota(jnp.int32, out.shape, 1)
    return jnp.where(point < length, out * scale, 0.0)


def synth_kernel(blocks, coef_ref, cos_ref, sin_ref, fc_ref, fs_ref, len_ref, scale_ref, out_ref):
    out_ref[...] = synthesize(
        coef_ref[...].astype(F32),
        cos_ref[3 * RADIX : 3 * RADIX + blocks, :],
        sin_ref[3 * RADIX : 3 * RADIX + blocks, :],
        fc_ref,
        fs_ref,
        len_ref[0],
        scale_ref[0],
    ).astype(BF16)


def gather_block(b, table, row_ref, col_ref, weight_ref, fields, blocks):
    stencil = col_ref.shape[0]
    half = 256
    lanes = pl.ds(pl.multiple_of(b * BLOCK, BLOCK), BLOCK)
    iota_half = lax.broadcasted_iota(jnp.int32, (half, BLOCK), 0).astype(F32).astype(BF16)
    iota_rows = lax.broadcasted_iota(jnp.int32, (3 * blocks, BLOCK), 0)
    one = jnp.ones((), BF16)
    zero = jnp.zeros((), BF16)
    acc = [jnp.zeros((blocks, BLOCK), F32) for _ in range(fields)]
    for p in range(stencil):
        col = col_ref[pl.ds(p, 1), lanes]
        row = row_ref[pl.ds(p, 1), lanes]
        weight = weight_ref[pl.ds(p, 1), lanes]
        point = col % BLOCK
        halves = []
        for h in range(BLOCK // half):
            local = point - h * half
            key = jnp.where((local >= 0) & (local < half), local, -1).astype(F32).astype(BF16)
            halves.append(jnp.where(iota_half == key, one, zero))
        onehot = jnp.concatenate(halves, axis=0)
        found = jnp.dot(table, onehot, preferred_element_type=F32)
        which = (row + 1) * blocks + col // BLOCK
        chosen = jnp.where(iota_rows == which, weight, 0.0)
        for r in range(3):
            sel = chosen[r * blocks : (r + 1) * blocks]
            for v in range(fields):
                start = (r * fields + v) * blocks
                acc[v] = acc[v] + found[start : start + blocks] * sel
    return [jnp.sum(a, axis=0, keepdims=True) for a in acc]


def advance(table_ref, row_ref, col_ref, weight_ref, new_ref, length, fields, blocks, real_blocks):
    new_ref[...] = jnp.zeros_like(new_ref)
    table = table_ref[...]

    def body(b, carry):
        interp = gather_block(b, table, row_ref, col_ref, weight_ref, fields, blocks)
        point = b * BLOCK + lax.broadcasted_iota(jnp.int32, (1, BLOCK), 1)
        for v in range(fields):
            value = interp[v] + 0.5 * interp[(v + 1) % fields] * jnp.tanh(interp[(v + 2) % fields])
            new_ref[pl.ds(v * blocks + b, 1), :] = jnp.where(point < length, value, 0.0)
        return carry

    lax.fori_loop(0, real_blocks, body, 0)


def analyse(new_ref, cos_block, sin_block, fc_ref, fs_ref, scale):
    blocks = cos_block.shape[0]
    fields = new_ref.shape[0] // blocks
    newgrid = new_ref[...].astype(BF16)
    part_real = jnp.dot(newgrid, fc_ref[...], preferred_element_type=F32)
    part_imag = jnp.dot(newgrid, fs_ref[...], preferred_element_type=F32)
    out = []
    for v in range(fields):
        pr = part_real[v * blocks : (v + 1) * blocks]
        pi = part_imag[v * blocks : (v + 1) * blocks]
        real = jnp.sum(pr * cos_block + pi * sin_block, axis=0, keepdims=True)
        imag = jnp.sum(pi * cos_block - pr * sin_block, axis=0, keepdims=True)
        out += [real * scale, imag * scale]
    return out


def grid_kernel(
    fields, blocks, real_blocks,
    table_ref, row_ref, col_ref, weight_ref, cos_ref, sin_ref, fc_ref, fs_ref, len_ref, scale_ref,
    out_ref, new_ref,
):
    advance(
        table_ref, row_ref, col_ref, weight_ref, new_ref, len_ref[0], fields, blocks, real_blocks
    )
    rows = analyse(
        new_ref,
        cos_ref[3 * RADIX : 3 * RADIX + blocks, :],
        sin_ref[3 * RADIX : 3 * RADIX + blocks, :],
        fc_ref,
        fs_ref,
        scale_ref[0],
    )
    out_ref[...] = jnp.concatenate(rows, axis=0).astype(BF16)


def per_device(
    spectrum,
    legendre,
    order_of_slot,
    reduced_length,
    gauss_weight,
    depart_row,
    depart_col,
    depart_weight,
):
    own_index = lax.axis_index("wave")
    count = lax.axis_size("wave")
    slot_count = legendre.shape[0]
    orders_total = order_of_slot.shape[0]
    variables, level_count = spectrum.shape[:2]
    assert level_count == 1
    steps = depart_row.shape[0]
    grid_width = depart_row.shape[-1]
    stencil = depart_row.shape[2]
    fields = variables
    real_blocks = grid_width // BLOCK
    blocks = padded_blocks(grid_width)

    own_orders = lax.dynamic_slice_in_dim(order_of_slot, own_index * slot_count, slot_count)
    degrees = jnp.arange(legendre.shape[2], dtype=jnp.int32)
    masked = jnp.where(
        degrees[None, None, :] >= own_orders[:, None, None], legendre, jnp.zeros((), BF16)
    )
    length = lax.dynamic_index_in_dim(reduced_length, own_index, keepdims=False)
    order_limit = jnp.minimum(orders_total, (length - 1) // 2)
    cos_rows, sin_rows = phase_rows(length, order_of_slot, blocks)
    active = (order_of_slot < order_limit).astype(F32)[None, :]
    fc, fs = pl.pallas_call(
        table_kernel,
        out_shape=[jax.ShapeDtypeStruct((BLOCK, orders_total), BF16)] * 2,
        in_specs=[VMEM_SPEC] * 3,
        out_specs=[VMEM_SPEC] * 2,
        scratch_shapes=[pltpu.VMEM((RADIX * RADIX, orders_total), F32)] * 2,
        name="table",
    )(cos_rows, sin_rows, active)
    length1 = length.reshape(1)
    grid_scale = (1.0 / jnp.sqrt(order_limit.astype(F32))).reshape(1)
    coef_scale = (gauss_weight[0] * jnp.sqrt(2.0 / length.astype(F32))).reshape(1)

    synth = pl.pallas_call(
        functools.partial(synth_kernel, blocks),
        out_shape=jax.ShapeDtypeStruct((fields * blocks, BLOCK), BF16),
        in_specs=[VMEM_SPEC] * 5 + [SMEM_SPEC] * 2,
        out_specs=VMEM_SPEC,
        name="synth",
    )
    grid_step = pl.pallas_call(
        functools.partial(grid_kernel, fields, blocks, real_blocks),
        out_shape=jax.ShapeDtypeStruct((2 * fields, orders_total), BF16),
        in_specs=[VMEM_SPEC] * 8 + [SMEM_SPEC] * 2,
        out_specs=VMEM_SPEC,
        scratch_shapes=[pltpu.VMEM((fields * blocks, BLOCK), F32)],
        name="grid_step",
    )
    spectral = spectrum.reshape(2 * fields, slot_count, -1)
    fourier = jnp.einsum("vsn,sjn->jvs", spectral, masked, preferred_element_type=F32)
    gram = jnp.einsum("sjn,skn->sjk", masked, masked, preferred_element_type=F32)
    forward = [(i, i + 1) for i in range(count - 1)]
    backward = [(i + 1, i) for i in range(count - 1)]
    for k in range(steps):
        gathered = lax.all_to_all(fourier.astype(BF16), "wave", split_axis=0, concat_axis=2, tiled=True)
        own = synth(
            gathered.reshape(2 * fields, orders_total), cos_rows, sin_rows, fc, fs, length1, grid_scale
        )
        low = lax.ppermute(own, "wave", forward)
        high = lax.ppermute(own, "wave", backward)
        coeffs = grid_step(
            jnp.concatenate([low, own, high], axis=0),
            depart_row[k].reshape(stencil, grid_width),
            depart_col[k].reshape(stencil, grid_width),
            depart_weight[k].reshape(stencil, grid_width),
            cos_rows, sin_rows, fc, fs, length1, coef_scale,
        )
        returned = lax.all_to_all(
            coeffs.reshape(1, 2 * fields, orders_total), "wave", split_axis=2, concat_axis=0, tiled=True
        )
        if k + 1 < steps:
            fourier = jnp.einsum("jvs,sjk->kvs", returned.astype(F32), gram, precision="highest")
    final = jnp.einsum("jvs,sjn->vsn", returned, masked, preferred_element_type=F32).astype(BF16)
    return final.reshape(spectrum.shape)


def solution(mesh):
    placed = (
        P(None, "lev", None, "wave", None),
        P("wave", None, None),
        P(),
        P(),
        P("wave"),
        P(None, "lev", None, "wave", None),
        P(None, "lev", None, "wave", None),
        P(None, "lev", None, "wave", None),
    )
    return jax.shard_map(
        per_device,
        mesh=mesh,
        in_specs=placed,
        out_specs=P(None, "lev", None, "wave", None),
        check_vma=False,
    )
```

time: 357 us -> 164 us (0.46)
  local copies, waits for them, and re-layouts: 209 us -> 37.8 us
  other arithmetic: 78.6 us -> 27 us
  Pallas kernels: 0 us -> 33.8 us
  waiting for transfers between devices: 8.07 us -> 0.02 us
  starting transfers between devices: 16.7 us -> 21.7 us
    gather x2 -> x0, local copies, waits for them, and re-layouts: 156 us -> none  [per_device(): values = jnp.take(flat_rows, flat_index, axis=1)]
    another operation x5 -> x0, other arithmetic: 38.4 us -> none
    pallas_call x0 -> x5, Pallas kernels: none -> 33.8 us  [the longest x2 22 us: per_device(): grid_step(jnp.concatenate([low, own, high], axis=0), depart_row[k].reshap...]
    select_n x2 -> x0, other arithmetic: 25.7 us -> none  [per_device(): values = jnp.take(flat_rows, flat_index, axis=1)]
    unnamed x0 -> x2, other arithmetic: none -> 18.2 us
    convert_element_type x9 -> x2, local copies, waits for them, and re-layouts: 19 us -> 3.56 us  [per_device(): fourier.astype(BF16)]
    concatenate x8 -> x0, local copies, waits for them, and re-layouts: 10.5 us -> none  [the longest x6 10.4 us: per_device(): jnp.roll(interp, -1, axis=0)]
    reduce_sum x4 -> x0, other arithmetic: 8.16 us -> none  [the longest x2 7.79 us: per_device(): interp = jnp.sum(values * weights[None], axis=2)]
  transfers between devices with their start and end apart: 6 -> 6, of which waited for: 3 -> 0; matrix products, arithmetic and copies ran while one was open for 12% -> 12% of each run, Pallas kernels for 0% -> 2%
where the time goes in v1:
time: 164 us; the launch traced here: 162 us
  local copies, waits for them, and re-layouts  37.8 us (23%)
  Pallas kernels  33.8 us (21%)
  other arithmetic  27 us (16%)
  starting transfers between devices  21.7 us (13%)
  blocking collectives  20.8 us (13%)
  matrix products  17.9 us (11%)
  between operations  3.19 us (2%)
    pallas_call x2, Pallas kernels, per_device(): grid_step(jnp.concatenate([low, own, high], axis=0), depart_row[k].reshap...  22 us
    unnamed x2, other arithmetic  18.2 us
    all_to_all x1, blocking collectives, per_device(): lax.all_to_all(fourier.astype(BF16), 'wave', split_axis=0, concat_axis=2,...  10.8 us
    unnamed x19, local copies, waits for them, and re-layouts  10.2 us
    all_to_all x1, blocking collectives, per_device(): lax.all_to_all(coeffs.reshape(1, 2 * fields, orders_total), 'wave', split...  9.99 us
    pallas_call x2, Pallas kernels, per_device(): synth(gathered.reshape(2 * fields, orders_total), cos_rows, sin_rows, fc,...  8 us
    all_to_all x6, local copies, waits for them, and re-layouts, per_device(): lax.all_to_all(coeffs.reshape(1, 2 * fields, orders_total), 'wave', split...  7.32 us
    ppermute x2, starting transfers between devices, per_device(): low = lax.ppermute(own, 'wave', forward)  6.91 us
  transfers between devices with their start and end apart: 6, of which 0 were waited for; matrix products, arithmetic and copies ran while one was open for 12% of the time, Pallas kernels for 2%

profile of v1, /device:TPU:0, one launch (start us, length us, event | category | flops | bytes accessed | tf_op | source)
XLA Modules:
  0.0 162.2 jit_solution(16123538923702126125)
XLA Ops:
  0.0 0.9 dynamic_slice.7
  1.1 0.8 copy-done
  1.9 0.7 copy-done.2
  2.6 5.5 %fusion.11 = bf16[8,8,160]{1,0,2:T(8,128)(2,1)} fusion(bf16[8,160,1280]{2,1,0:T(8,128)(2,1)S(1)} %bitcast.54, bf16[160,8,1280]{2,1,0:T(8,128)(2,1)} %param.9, pred[160,1280]{1,0:T(8,128)(4,1)S(1)} %iota_compare_fusion), kind=kOutput, calls=%fused_computation.12 | convolution fusion | flops 27863040 | bytes 6778880 | tf_op jit(solution)/shard_map/vsn,sjn->jvs/dot_general | solution.py:235
  8.1 1.8 %copy.36 = bf16[8,8,160]{2,1,0:T(8,128)(2,1)} copy(bf16[8,8,160]{1,0,2:T(8,128)(2,1)} %fusion.11) | data formatting | bytes 40960 | tf_op jit(solution)/shard_map/convert_element_type | solution.py:240
  9.9 6.4 %all-to-all-start = ((bf16[8,8,160]{2,1,0:T(8,128)(2,1)}), bf16[8,8,160]{2,1,0:T(8,128)(2,1)}, u32[]{:S(2)}, u32[]{:S(2)}) async-start(bf16[8,8,160]{2,1,0:T(8,128)(2,1)} %copy.36), calls=%async_computation | async-start | bytes 65536 | tf_op jit(solution)/shard_map/all_to_all | solution.py:240
  20.2 1.0 fusion.29
  21.2 1.6 fusion.28
  22.8 0.7 copy_bitcast_fusion.4
  23.5 0.8 pad_add_fusion
  24.3 3.6 %fusion.20 = (f32[40,1280]{1,0:T(8,128)}, f32[40,1280]{1,0:T(8,128)}) fusion(f32[]{:T(128)S(6)} %div.15, s32[]{:T(128)S(6)} %select_n.27, s32[1280]{0:T(1024)S(1)} %copy-done.4, s32[40]{0:T(128)S(1)} %pad_add_fusion, pred[]{:T(512)S(6)} %lt.24), kind=kLoop, calls=%fused_computation.22 | loop fusion | flops 512000 | bytes 414889 | tf_op jit(solution)/shard_map/sin | solution.py:32
  28.5 3.8 %table.1 = (bf16[512,1280]{1,0:T(8,128)(2,1)}, bf16[512,1280]{1,0:T(8,128)(2,1)}) custom-call(f32[40,1280]{1,0:T(8,128)} %get-tuple-element.16.cos_ref, f32[40,1280]{1,0:T(8,128)} %get-tuple-element.15.sin_ref, f32[1,1280]{1,0:T(1,128)} %reshape.58.active_ref), custom_call_target="tpu_custom_call" | custom-call | tf_op jit(solution)/shard_map/table/pallas_call | solution.py:207
  32.3 0.8 copy.37
  33.0 0.7 reshape.51.coef_ref
  33.7 4.0 %synth.2 = bf16[64,512]{1,0:T(8,128)(2,1)} custom-call(bf16[8,1280]{1,0:T(8,128)(2,1)} %reshape.51.coef_ref, f32[40,1280]{1,0:T(8,128)} %get-tuple-element.16.cos_ref, f32[40,1280]{1,0:T(8,128)} %get-tuple-element.15.sin_ref, bf16[512,1280]{1,0:T(8,128)(2,1)} %get-tuple-element.7.fc_ref, bf16[512,1280]{1,0:T(8,128)(2,1)} %get-tuple-element.8.fs_ref, ...), custom_call_target="tpu_custom_call" | custom-call | tf_op jit(solution)/shard_map/synth/pallas_call | solution.py:241
  37.7 1.3 collective-permute-start.1
  39.0 3.7 %collective-permute-start = (bf16[64,512]{1,0:T(8,128)(2,1)}, bf16[64,512]{1,0:T(8,128)(2,1)}, u32[]{:S(2)}, u32[]{:S(2)}) collective-permute-start(bf16[64,512]{1,0:T(8,128)(2,1)} %synth.2), channel_id=1, source_target_pairs={{0,4},{4,8},{8,12},{12,16},{16,20},{20,24},{24,28},{1,5},{5,9},{9,... | collective-permute-start | bytes 196616 | tf_op jit(solution)/shard_map/ppermute | solution.py:244
  42.7 0.9 fusion.27
  45.0 1.6 pad_maximum_fusion.table_ref
  46.6 11.0 %grid_step.2 = bf16[8,1280]{1,0:T(8,128)(2,1)} custom-call(bf16[192,512]{1,0:T(8,128)(2,1)} %pad_maximum_fusion.table_ref, s32[4,5632]{1,0:T(4,128)} %get-tuple-element.20.row_ref, s32[4,5632]{1,0:T(4,128)} %get-tuple-element.19.col_ref, f32[4,5632]{1,0:T(4,128)} %bitcast.60, f32[40,1280]{1,0:T(8,128)} %get-tuple-element.16.cos_ref, ...), custom_call_target="tpu_custom_call" | custom-call | tf_op jit(solution)/shard_map/grid_step/pallas_call | solution.py:246
  57.6 1.9 %copy.41 = bf16[1,8,1280]{1,0,2:T(2,128)(2,1)} copy(bf16[1,8,1280]{2,1,0:T(8,128)(2,1)} %bitcast.63) | data formatting | bytes 40960 | tf_op jit(solution)/shard_map/reshape | solution.py:254
  60.0 9.1 %reduce = bf16[1280,8]{1,0:T(8,128)(2,1)} reduce(bf16[1280,1,8]{2,1,0:T(2,128)(2,1)} %bitcast.55, bf16[]{:T(256)} %broadcast.29), dimensions={1}, to_apply=%bitcast.46.reduce_sub_computation | reduce | bytes 40962
  69.1 1.9 %reshape.59 = bf16[8,2,640]{2,1,0:T(2,128)(2,1)} reshape(bf16[1280,8]{1,0:T(8,128)(2,1)} %reduce) | data formatting | bytes 40960
  71.0 5.9 %all-to-all-start.1 = ((bf16[8,2,640]{2,1,0:T(2,128)(2,1)}), bf16[8,2,640]{2,1,0:T(2,128)(2,1)}, u32[]{:S(2)}, u32[]{:S(2)}) async-start(bf16[8,2,640]{2,1,0:T(2,128)(2,1)} %reshape.59), calls=%async_computation.1 | async-start | bytes 40960 | tf_op jit(solution)/shard_map/all_to_all | solution.py:253
  76.9 6.6 %fusion.3 = f32[160,8,8]{1,2,0:T(8,128)} fusion(bf16[160,8,1280]{2,1,0:T(8,128)(2,1)} %param.9, pred[160,1280]{1,0:T(8,128)(4,1)} %copy-done.2), kind=kOutput, calls=%fused_computation.5 | convolution fusion | flops 27852800 | bytes 3522560 | tf_op jit(solution)/shard_map/sjn,skn->sjk/dot_general | solution.py:236
  83.5 2.2 %reshape.60 = bf16[1280,1,8]{2,1,0:T(2,128)(2,1)} reshape(bf16[8,2,640]{2,1,0:T(2,128)(2,1)} %all-to-all-done.1) | data formatting | bytes 40960
  85.7 1.8 %copy.42 = bf16[1,8,1280]{2,1,0:T(8,128)(2,1)} copy(bf16[1,8,1280]{1,0,2:T(2,128)(2,1)} %bitcast.57) | data formatting | bytes 40960 | tf_op jit(solution)/shard_map/all_to_all | solution.py:253
  87.5 1.4 all_to_all.52
  89.0 1.8 %copy.43 = bf16[1,8,8,160]{1,2,3,0:T(8,128)(2,1)} copy(bf16[1,8,8,160]{3,2,1,0:T(8,128)(2,1)} %all_to_all.52) | data formatting | bytes 40960 | tf_op jit(solution)/shard_map/all_to_all | solution.py:253
  90.7 2.6 %fusion.10 = bf16[8,8,160]{1,0,2:T(8,128)(2,1)} fusion(f32[160,8,8]{1,2,0:T(8,128)} %fusion.3, bf16[1,8,8,160]{1,2,3,0:T(8,128)(2,1)} %copy.43), kind=kOutput, calls=%fused_computation.11 | convolution fusion | flops 993280 | bytes 81920 | tf_op jit(solution)/shard_map/jvs,sjk->kvs/dot_general | solution.py:257
  93.3 1.8 %copy.45 = bf16[8,8,160]{2,1,0:T(8,128)(2,1)} copy(bf16[8,8,160]{1,0,2:T(8,128)(2,1)} %fusion.10) | data formatting | bytes 40960 | tf_op jit(solution)/shard_map/convert_element_type | solution.py:240
  95.1 10.8 %all_to_all.66 = bf16[8,8,160]{2,1,0:T(8,128)(2,1)S(1)} all-to-all(bf16[8,8,160]{2,1,0:T(8,128)(2,1)} %copy.45), channel_id=1, replica_groups=mesh['wave'=8,'lev'=4] {'wave'}, dimensions={0} | all-to-all | bytes 40960 | tf_op jit(solution)/shard_map/all_to_all | solution.py:240
  106.5 1.5 reshape.55.coef_ref
  108.0 4.0 %synth.3 = bf16[64,512]{1,0:T(8,128)(2,1)} custom-call(bf16[8,1280]{1,0:T(8,128)(2,1)} %reshape.55.coef_ref, f32[40,1280]{1,0:T(8,128)} %get-tuple-element.16.cos_ref, f32[40,1280]{1,0:T(8,128)} %get-tuple-element.15.sin_ref, bf16[512,1280]{1,0:T(8,128)(2,1)} %get-tuple-element.7.fc_ref, bf16[512,1280]{1,0:T(8,128)(2,1)} %get-tuple-element.8.fs_ref, ...), custom_call_target="tpu_custom_call" | custom-call | tf_op jit(solution)/shard_map/synth/pallas_call | solution.py:241
  112.0 1.3 collective-permute-start.3
  113.3 3.3 %collective-permute-start.2 = (bf16[64,512]{1,0:T(8,128)(2,1)}, bf16[64,512]{1,0:T(8,128)(2,1)S(1)}, u32[]{:S(2)}, u32[]{:S(2)}) collective-permute-start(bf16[64,512]{1,0:T(8,128)(2,1)} %synth.3), channel_id=1, source_target_pairs={{0,4},{4,8},{8,12},{12,16},{16,20},{20,24},{24,28},{1,5},{5,9},{9,... | collective-permute-start | bytes 196616 | tf_op jit(solution)/shard_map/ppermute | solution.py:244
  116.6 0.7 copy_bitcast_fusion.1
  118.0 1.5 pad_maximum_fusion.1.table_ref
  119.5 11.0 %grid_step.3 = bf16[8,1280]{1,0:T(8,128)(2,1)} custom-call(bf16[192,512]{1,0:T(8,128)(2,1)} %pad_maximum_fusion.1.table_ref, s32[4,5632]{1,0:T(4,128)} %get-tuple-element.22.row_ref, s32[4,5632]{1,0:T(4,128)} %get-tuple-element.21.col_ref, f32[4,5632]{1,0:T(4,128)} %bitcast.59, f32[40,1280]{1,0:T(8,128)} %get-tuple-element.16.cos_ref, ...), custom_call_target="tpu_custom_call" | custom-call | tf_op jit(solution)/shard_map/grid_step/pallas_call | solution.py:246
  130.5 1.9 %copy.50 = bf16[1,8,1280]{1,0,2:T(2,128)(2,1)} copy(bf16[1,8,1280]{2,1,0:T(8,128)(2,1)} %bitcast.62) | data formatting | bytes 40960 | tf_op jit(solution)/shard_map/reshape | solution.py:254
  132.4 9.1 %reduce.1 = bf16[1280,8]{1,0:T(8,128)(2,1)} reduce(bf16[1280,1,8]{2,1,0:T(2,128)(2,1)} %bitcast.56, bf16[]{:T(256)} %broadcast.29), dimensions={1}, to_apply=%bitcast.48.reduce_sub_computation | reduce | bytes 40962
  141.5 1.3 reshape.61
  142.8 10.0 %all_to_all.67 = bf16[8,2,640]{2,1,0:T(2,128)(2,1)S(1)} all-to-all(bf16[8,2,640]{2,1,0:T(2,128)(2,1)S(1)} %reshape.61), channel_id=1, replica_groups=mesh['wave'=8,'lev'=4] {'wave'}, dimensions={0} | all-to-all | bytes 40960 | tf_op jit(solution)/shard_map/all_to_all | solution.py:253
  152.8 1.5 reshape.62
  154.3 1.2 copy.51
  155.6 0.9 copy.52
  156.6 3.3 %fusion = bf16[8,160,1280]{2,0,1:T(8,128)(2,1)S(1)} fusion(bf16[160,8,1280]{2,1,0:T(8,128)(2,1)} %param.9, pred[160,1280]{1,0:T(8,128)(4,1)S(1)} %copy-done.3, bf16[1,8,8,160]{2,1,3,0:T(8,128)(2,1)} %copy.52), kind=kOutput, calls=%fused_computation.1 | convolution fusion | flops 29491200 | bytes 6778880 | tf_op jit(solution)/shard_map/jvs,sjn->vsn/dot_general | solution.py:258
  159.9 2.3 %copy.55 = bf16[8,160,1280]{2,1,0:T(8,128)(2,1)} copy(bf16[8,160,1280]{2,0,1:T(8,128)(2,1)S(1)} %fusion) | data formatting | bytes 6553600 | tf_op jit(solution)/shard_map/reshape | solution.py:259
  (28 shorter events, 5.1 us)
Async XLA Ops:
  0.0 1.9 %copy-start = (bf16[4,1,2,160,1280]{4,3,2,1,0:T(8,128)(2,1)S(1)}, bf16[4,1,2,160,1280]{4,3,2,1,0:T(8,128)(2,1)}, u32[]{:S(2)}) copy-start(bf16[4,1,2,160,1280]{4,3,2,1,0:T(8,128)(2,1)} %param.8) | copy-start | bytes 9830404
  1.9 0.7 copy-start.2
  2.6 13.6 %copy-start.5 = (s32[8]{0:T(128)S(1)}, s32[8]{0:T(128)}, u32[]{:S(2)}) copy-start(s32[8]{0:T(128)} %param.11) | copy-start | bytes 100
  2.6 21.7 %copy-start.4 = (s32[1280]{0:T(1024)S(1)}, s32[1280]{0:T(1024)}, u32[]{:S(2)}) copy-start(s32[1280]{0:T(1024)} %param.10) | copy-start | bytes 15364
  9.9 22.4 %all-to-all-start = ((bf16[8,8,160]{2,1,0:T(8,128)(2,1)}), bf16[8,8,160]{2,1,0:T(8,128)(2,1)}, u32[]{:S(2)}, u32[]{:S(2)}) async-start(bf16[8,8,160]{2,1,0:T(8,128)(2,1)} %copy.36), calls=%async_computation | async-start | bytes 65536 | tf_op jit(solution)/shard_map/all_to_all | solution.py:240
  37.7 7.3 %collective-permute-start.1 = (bf16[64,512]{1,0:T(8,128)(2,1)}, bf16[64,512]{1,0:T(8,128)(2,1)}, u32[]{:S(2)}, u32[]{:S(2)}) collective-permute-start(bf16[64,512]{1,0:T(8,128)(2,1)} %synth.2), channel_id=1, source_target_pairs={{4,0},{8,4},{12,8},{16,12},{20,16},{24,20},{28,24},{5,1},{9,5},{13... | collective-permute-start | bytes 196616 | tf_op jit(solution)/shard_map/ppermute | solution.py:245
  39.0 6.0 %collective-permute-start = (bf16[64,512]{1,0:T(8,128)(2,1)}, bf16[64,512]{1,0:T(8,128)(2,1)}, u32[]{:S(2)}, u32[]{:S(2)}) collective-permute-start(bf16[64,512]{1,0:T(8,128)(2,1)} %synth.2), channel_id=1, source_target_pairs={{0,4},{4,8},{8,12},{12,16},{16,20},{20,24},{24,28},{1,5},{5,9},{9,... | collective-permute-start | bytes 196616 | tf_op jit(solution)/shard_map/ppermute | solution.py:244
  71.0 12.5 %all-to-all-start.1 = ((bf16[8,2,640]{2,1,0:T(2,128)(2,1)}), bf16[8,2,640]{2,1,0:T(2,128)(2,1)}, u32[]{:S(2)}, u32[]{:S(2)}) async-start(bf16[8,2,640]{2,1,0:T(2,128)(2,1)} %reshape.59), calls=%async_computation.1 | async-start | bytes 40960 | tf_op jit(solution)/shard_map/all_to_all | solution.py:253
  83.5 33.1 %copy-start.1 = (s32[1,1,4,1,5632]{4,3,2,1,0:T(1,128)S(1)}, s32[1,1,4,1,5632]{4,3,2,1,0:T(1,128)}, u32[]{:S(2)}) copy-start(s32[1,1,4,1,5632]{4,3,2,1,0:T(1,128)} %get-tuple-element.11) | copy-start | bytes 270340
  112.0 5.9 %collective-permute-start.3 = (bf16[64,512]{1,0:T(8,128)(2,1)}, bf16[64,512]{1,0:T(8,128)(2,1)S(1)}, u32[]{:S(2)}, u32[]{:S(2)}) collective-permute-start(bf16[64,512]{1,0:T(8,128)(2,1)} %synth.3), channel_id=1, source_target_pairs={{4,0},{8,4},{12,8},{16,12},{20,16},{24,20},{28,24},{5,1},{9,5},{13... | collective-permute-start | bytes 196616 | tf_op jit(solution)/shard_map/ppermute | solution.py:245
  113.3 4.7 %collective-permute-start.2 = (bf16[64,512]{1,0:T(8,128)(2,1)}, bf16[64,512]{1,0:T(8,128)(2,1)S(1)}, u32[]{:S(2)}, u32[]{:S(2)}) collective-permute-start(bf16[64,512]{1,0:T(8,128)(2,1)} %synth.3), channel_id=1, source_target_pairs={{0,4},{4,8},{8,12},{12,16},{16,20},{20,24},{24,28},{1,5},{5,9},{9,... | collective-permute-start | bytes 196616 | tf_op jit(solution)/shard_map/ppermute | solution.py:244
  119.5 37.1 %copy-start.3 = (pred[160,1280]{1,0:T(8,128)(4,1)S(1)}, pred[160,1280]{1,0:T(8,128)(4,1)}, u32[]{:S(2)}) copy-start(pred[160,1280]{1,0:T(8,128)(4,1)} %copy-done.2) | copy-start | bytes 614404

commit v2 on v1

--- a/solution.py
+++ b/solution.py
@@ -32,7 +32,7 @@
     return jnp.cos(angles), jnp.sin(angles)
 
 
-def table_kernel(cos_ref, sin_ref, active_ref, fc_ref, fs_ref, ca_ref, sa_ref):
+def build_table(cos_ref, sin_ref, active_ref, fc_ref, fs_ref, ca_ref, sa_ref):
     active = active_ref[...]
     cos_low = cos_ref[0:RADIX, :] * active
     sin_low = sin_ref[0:RADIX, :] * active
@@ -91,8 +91,8 @@
     ).astype(BF16)
 
 
-def gather_block(b, table, row_ref, col_ref, weight_ref, fields, blocks):
-    stencil = col_ref.shape[0]
+def gather_block(b, k, table, row_ref, col_ref, weight_ref, fields, blocks):
+    stencil = col_ref.shape[1]
     half = 256
     lanes = pl.ds(pl.multiple_of(b * BLOCK, BLOCK), BLOCK)
     iota_half = lax.broadcasted_iota(jnp.int32, (half, BLOCK), 0).astype(F32).astype(BF16)
@@ -101,9 +101,9 @@
     zero = jnp.zeros((), BF16)
     acc = [jnp.zeros((blocks, BLOCK), F32) for _ in range(fields)]
     for p in range(stencil):
-        col = col_ref[pl.ds(p, 1), lanes]
-        row = row_ref[pl.ds(p, 1), lanes]
-        weight = weight_ref[pl.ds(p, 1), lanes]
+        col = col_ref[k, p, :, lanes]
+        row = row_ref[k, p, :, lanes]
+        weight = weight_ref[k, p, :, lanes]
         point = col % BLOCK
         halves = []
         for h in range(BLOCK // half):
@@ -122,12 +122,11 @@
     return [jnp.sum(a, axis=0, keepdims=True) for a in acc]
 
 
-def advance(table_ref, row_ref, col_ref, weight_ref, new_ref, length, fields, blocks, real_blocks):
+def advance(table, k, row_ref, col_ref, weight_ref, new_ref, length, fields, blocks, real_blocks):
     new_ref[...] = jnp.zeros_like(new_ref)
-    table = table_ref[...]
 
     def body(b, carry):
-        interp = gather_block(b, table, row_ref, col_ref, weight_ref, fields, blocks)
+        interp = gather_block(b, k, table, row_ref, col_ref, weight_ref, fields, blocks)
         point = b * BLOCK + lax.broadcasted_iota(jnp.int32, (1, BLOCK), 1)
         for v in range(fields):
             value = interp[v] + 0.5 * interp[(v + 1) % fields] * jnp.tanh(interp[(v + 2) % fields])
@@ -159,7 +158,8 @@
     out_ref, new_ref,
 ):
     advance(
-        table_ref, row_ref, col_ref, weight_ref, new_ref, len_ref[0], fields, blocks, real_blocks
+        table_ref[...], 0, row_ref, col_ref, weight_ref, new_ref, len_ref[0],
+        fields, blocks, real_blocks,
     )
     rows = analyse(
         new_ref,
@@ -170,6 +170,259 @@
         scale_ref[0],
     )
     out_ref[...] = jnp.concatenate(rows, axis=0).astype(BF16)
+
+
+GROUP = 16
+MESH = pl.DeviceIdType.MESH
+
+
+def forward_kernel(
+    fields, slots, rows_j,
+    orders_ref, spec_ref, leg_ref, send_ref, gram_ref, masked_ref, four_ref, gram_raw_ref, vjs_ref,
+):
+    g = pl.program_id(0)
+    groups = pl.num_programs(0)
+    first = lax.axis_index("wave") * slots + g * GROUP
+    degree = lax.broadcasted_iota(jnp.int32, (rows_j, leg_ref.shape[1]), 1)
+    for pair in range(GROUP // 2):
+        parts = []
+        for s in (2 * pair, 2 * pair + 1):
+            rows = leg_ref[s * rows_j : (s + 1) * rows_j, :].astype(F32)
+            parts.append(jnp.where(degree >= orders_ref[first + s], rows, 0.0))
+        masked_ref[2 * pair * rows_j : 2 * (pair + 1) * rows_j, :] = jnp.concatenate(
+            parts, axis=0
+        ).astype(BF16)
+    masked = masked_ref[...]
+    state = spec_ref[...].reshape(fields * GROUP, spec_ref.shape[2])
+    dims = (((1,), (1,)), ((), ()))
+    size = GROUP * rows_j
+    prod = lax.dot_general(masked, state, dims, preferred_element_type=F32)
+    row = lax.broadcasted_iota(jnp.int32, (size, fields * GROUP), 0) // rows_j
+    col = lax.broadcasted_iota(jnp.int32, (size, fields * GROUP), 1) % GROUP
+    prod = jnp.where(row == col, prod, 0.0)
+    four_ref[g] = jnp.sum(prod.reshape(GROUP, rows_j, fields * GROUP), axis=0)
+    square = lax.dot_general(masked, masked, dims, preferred_element_type=F32)
+    row = lax.broadcasted_iota(jnp.int32, (size, size), 0)
+    col = lax.broadcasted_iota(jnp.int32, (size, size), 1)
+    square = jnp.where(row // rows_j == col // rows_j, square, 0.0)
+    diag = jnp.sum(square.reshape(GROUP, rows_j, size), axis=0)
+    swap = (row // rows_j == col % GROUP) & (row % rows_j == col // GROUP)
+    gram_raw_ref[g] = jnp.dot(
+        diag, jnp.where(swap, 1.0, 0.0), preferred_element_type=F32, precision="highest"
+    )
+
+    @pl.when(g == groups - 1)
+    def _():
+        vjs_ref[...] = jnp.zeros_like(vjs_ref)
+        gram_ref[...] = jnp.zeros_like(gram_ref)
+        for h in range(slots // GROUP):
+            lanes = slice(h * GROUP, (h + 1) * GROUP)
+            for v in range(fields):
+                vjs_ref[v, :, lanes] = four_ref[h, :, v * GROUP : (v + 1) * GROUP]
+            for j in range(rows_j):
+                gram_ref[j, :, lanes] = gram_raw_ref[h, :, j * GROUP : (j + 1) * GROUP]
+        send_ref[...] = jnp.swapaxes(vjs_ref[...], 0, 1)
+
+
+def inverse_kernel(fields, rows_j, coef_ref, masked_ref, out_ref):
+    size = GROUP * rows_j
+    row = lax.broadcasted_iota(jnp.int32, (size, fields * GROUP), 0) // rows_j
+    col = lax.broadcasted_iota(jnp.int32, (size, fields * GROUP), 1) % GROUP
+    tiled = jnp.concatenate([coef_ref[0]] * GROUP, axis=0)
+    spread = jnp.where(row == col, tiled, 0.0).astype(BF16)
+    out = lax.dot_general(
+        spread, masked_ref[...], (((0,), (0,)), ((), ())), preferred_element_type=F32
+    )
+    out_ref[...] = out.astype(BF16).reshape(out_ref.shape)
+
+
+def steps_kernel(
+    steps, count, fields, blocks, real_blocks, slots,
+    first_ref, gram_ref, cos_ref, sin_ref, active_ref, row_ref, col_ref, weight_ref,
+    len_ref, grid_scale_ref, coef_scale_ref,
+    out_ref,
+    fc_ref, fs_ref, ca_ref, sa_ref, spec_send, spec_recv, grid_send, grid_recv, tab_ref, coef_ref,
+    new_ref, spec_ssem, spec_rsem, grid_ssem, grid_rsem, halo_ssem, halo_rsem,
+):
+    tab_ref[...] = jnp.zeros_like(tab_ref)
+    grid_send[...] = jnp.zeros_like(grid_send)
+    me = lax.axis_index("wave")
+    peers = [lax.rem(me + d, count) for d in range(1, count)]
+    barrier = pltpu.get_barrier_semaphore()
+    for peer in peers:
+        pl.semaphore_signal(barrier, inc=1, device_id={"wave": peer}, device_id_type=MESH)
+    pl.semaphore_wait(barrier, count - 1)
+
+    def exchange(send, recv, ssem, rsem):
+        copies = []
+        for d, peer in enumerate(peers):
+            copy = pltpu.make_async_remote_copy(
+                src_ref=send.at[peer], dst_ref=recv.at[me], send_sem=ssem.at[d],
+                recv_sem=rsem.at[d], device_id={"wave": peer}, device_id_type=MESH,
+            )
+            copy.start()
+            copies.append(copy)
+        return copies
+
+    copies = exchange(first_ref, spec_recv.at[0], spec_ssem.at[0], spec_rsem.at[0])
+    build_table(cos_ref, sin_ref, active_ref, fc_ref, fs_ref, ca_ref, sa_ref)
+    cos_block = cos_ref[3 * RADIX : 3 * RADIX + blocks, :]
+    sin_block = sin_ref[3 * RADIX : 3 * RADIX + blocks, :]
+    rows = fields // 2 * blocks
+    for k in range(steps):
+        source = first_ref if k == 0 else spec_send.at[k - 1]
+        for copy in copies:
+            copy.wait()
+        spec_recv[k, me] = source[me]
+        for i in range(count):
+            coef_ref[:, i * slots : (i + 1) * slots] = spec_recv[k, i, :, :slots]
+        own = synthesize(
+            coef_ref[...], cos_block, sin_block, fc_ref, fs_ref, len_ref[0], grid_scale_ref[0]
+        )
+        tab_ref[k, 1] = own.astype(BF16)
+        up = pltpu.make_async_remote_copy(
+            src_ref=tab_ref.at[k, 1], dst_ref=tab_ref.at[k, 0], send_sem=halo_ssem.at[k, 0],
+            recv_sem=halo_rsem.at[k, 0], device_id={"wave": lax.rem(me + 1, count)},
+            device_id_type=MESH,
+        )
+        down = pltpu.make_async_remote_copy(
+            src_ref=tab_ref.at[k, 1], dst_ref=tab_ref.at[k, 2], send_sem=halo_ssem.at[k, 1],
+            recv_sem=halo_rsem.at[k, 1], device_id={"wave": lax.rem(me + count - 1, count)},
+            device_id_type=MESH,
+        )
+
+        @pl.when(me < count - 1)
+        def _():
+            up.start()
+
+        @pl.when(me > 0)
+        def _():
+            down.start()
+            up.wait_recv()
+
+        @pl.when(me < count - 1)
+        def _():
+            down.wait_recv()
+
+        table = tab_ref[k].reshape(3 * rows, BLOCK)
+        advance(
+            table, k, row_ref, col_ref, weight_ref, new_ref, len_ref[0],
+            fields // 2, blocks, real_blocks,
+        )
+
+        @pl.when(me < count - 1)
+        def _():
+            up.wait_send()
+
+        @pl.when(me > 0)
+        def _():
+            down.wait_send()
+
+        parts = analyse(new_ref, cos_block, sin_block, fc_ref, fs_ref, coef_scale_ref[0])
+        for v, part in enumerate(parts):
+            coef_ref[v : v + 1, :] = part
+        for i in range(count):
+            grid_send[k, i, :, :slots] = coef_ref[:, i * slots : (i + 1) * slots]
+        copies = exchange(grid_send.at[k], grid_recv.at[k], grid_ssem.at[k], grid_rsem.at[k])
+        grid_recv[k, me] = grid_send[k, me]
+        for copy in copies:
+            copy.wait()
+        if k + 1 < steps:
+            mixed = []
+            for v in range(fields):
+                total = None
+                for j in range(count):
+                    term = gram_ref[j] * grid_recv[k, j, v : v + 1, :]
+                    total = term if total is None else total + term
+                mixed.append(total[None])
+            spec_send[k] = jnp.swapaxes(jnp.concatenate(mixed, axis=0), 0, 1)
+            copies = exchange(
+                spec_send.at[k], spec_recv.at[k + 1], spec_ssem.at[k + 1], spec_rsem.at[k + 1]
+            )
+    last = jnp.swapaxes(grid_recv[steps - 1], 0, 1)
+    for h in range(slots // GROUP):
+        for v in range(fields):
+            out_ref[h, :, v * GROUP : (v + 1) * GROUP] = last[v, :, h * GROUP : (h + 1) * GROUP]
+
+
+def fused(spectrum, legendre, order_of_slot, length, gauss_weight, row, col, weight, count):
+    slots, rows_j, degrees = legendre.shape
+    fields = 2 * spectrum.shape[0]
+    orders_total = order_of_slot.shape[0]
+    steps, stencil, grid_width = row.shape[0], row.shape[2], row.shape[-1]
+    real_blocks = grid_width // BLOCK
+    blocks = padded_blocks(grid_width)
+    groups = slots // GROUP
+    size = GROUP * rows_j
+    lanes = -(-slots // 128) * 128
+    order_limit = jnp.minimum(orders_total, (length - 1) // 2)
+    cos_rows, sin_rows = phase_rows(length, order_of_slot, blocks)
+    active = (order_of_slot < order_limit).astype(F32)[None, :]
+    grid_scale = (1.0 / jnp.sqrt(order_limit.astype(F32))).reshape(1)
+    coef_scale = (gauss_weight[0] * jnp.sqrt(2.0 / length.astype(F32))).reshape(1)
+    send, gram, masked = pl.pallas_call(
+        functools.partial(forward_kernel, fields, slots, rows_j),
+        grid=(groups,),
+        out_shape=[
+            jax.ShapeDtypeStruct((rows_j, fields, lanes), F32),
+            jax.ShapeDtypeStruct((rows_j, rows_j, lanes), F32),
+            jax.ShapeDtypeStruct((slots * rows_j, degrees), BF16),
+        ],
+        in_specs=[
+            SMEM_SPEC,
+            pl.BlockSpec((fields, GROUP, degrees), lambda g: (0, g, 0)),
+            pl.BlockSpec((size, degrees), lambda g: (g, 0)),
+        ],
+        out_specs=[
+            pl.BlockSpec((rows_j, fields, lanes), lambda g: (0, 0, 0)),
+            pl.BlockSpec((rows_j, rows_j, lanes), lambda g: (0, 0, 0)),
+            pl.BlockSpec((size, degrees), lambda g: (g, 0)),
+        ],
+        scratch_shapes=[
+            pltpu.VMEM((groups, rows_j, fields * GROUP), F32),
+            pltpu.VMEM((groups, rows_j, size), F32),
+            pltpu.VMEM((fields, rows_j, lanes), F32),
+        ],
+        name="forward",
+    )(order_of_slot, spectrum.reshape(fields, slots, degrees), legendre.reshape(slots * rows_j, degrees))
+    shape = (steps, count, fields, lanes)
+    table_rows = fields // 2 * blocks
+    coeffs = pl.pallas_call(
+        functools.partial(steps_kernel, steps, count, fields, blocks, real_blocks, slots),
+        out_shape=jax.ShapeDtypeStruct((groups, rows_j, fields * GROUP), F32),
+        in_specs=[VMEM_SPEC] * 8 + [SMEM_SPEC] * 3,
+        out_specs=VMEM_SPEC,
+        scratch_shapes=[pltpu.VMEM((BLOCK, orders_total), BF16)] * 2
+        + [pltpu.VMEM((RADIX * RADIX, orders_total), F32)] * 2
+        + [pltpu.VMEM(shape, F32)] * 4
+        + [
+            pltpu.VMEM((steps, 3, table_rows, BLOCK), BF16),
+            pltpu.VMEM((fields, orders_total), F32),
+            pltpu.VMEM((table_rows, BLOCK), F32),
+        ]
+        + [pltpu.SemaphoreType.DMA((steps, count - 1))] * 4
+        + [pltpu.SemaphoreType.DMA((steps, 2))] * 2,
+        compiler_params=pltpu.CompilerParams(collective_id=0, has_side_effects=True),
+        name="steps",
+    )(
+        send, gram, cos_rows, sin_rows, active,
+        row.reshape(steps, stencil, 1, grid_width),
+        col.reshape(steps, stencil, 1, grid_width),
+        weight.reshape(steps, stencil, 1, grid_width),
+        length.reshape(1), grid_scale, coef_scale,
+    )
+    out = pl.pallas_call(
+        functools.partial(inverse_kernel, fields, rows_j),
+        grid=(groups,),
+        out_shape=jax.ShapeDtypeStruct((fields, slots, degrees), BF16),
+        in_specs=[
+            pl.BlockSpec((1, rows_j, fields * GROUP), lambda g: (g, 0, 0)),
+            pl.BlockSpec((size, degrees), lambda g: (g, 0)),
+        ],
+        out_specs=pl.BlockSpec((fields, GROUP, degrees), lambda g: (0, g, 0)),
+        name="inverse",
+    )(coeffs, masked)
+    return out.reshape(spectrum.shape)
 
 
 def per_device(
@@ -195,17 +448,24 @@
     real_blocks = grid_width // BLOCK
     blocks = padded_blocks(grid_width)
 
+    length = lax.dynamic_index_in_dim(reduced_length, own_index, keepdims=False)
+    fits = slot_count % GROUP == 0 and 2 * fields == 8
+    if fits and legendre.shape[1] == 8 and count == 8:
+        return fused(
+            spectrum, legendre, order_of_slot, length, gauss_weight,
+            depart_row, depart_col, depart_weight, count,
+        )
+
     own_orders = lax.dynamic_slice_in_dim(order_of_slot, own_index * slot_count, slot_count)
     degrees = jnp.arange(legendre.shape[2], dtype=jnp.int32)
     masked = jnp.where(
         degrees[None, None, :] >= own_orders[:, None, None], legendre, jnp.zeros((), BF16)
     )
-    length = lax.dynamic_index_in_dim(reduced_length, own_index, keepdims=False)
     order_limit = jnp.minimum(orders_total, (length - 1) // 2)
     cos_rows, sin_rows = phase_rows(length, order_of_slot, blocks)
     active = (order_of_slot < order_limit).astype(F32)[None, :]
     fc, fs = pl.pallas_call(
-        table_kernel,
+        build_table,
         out_shape=[jax.ShapeDtypeStruct((BLOCK, orders_total), BF16)] * 2,
         in_specs=[VMEM_SPEC] * 3,
         out_specs=[VMEM_SPEC] * 2,
@@ -245,9 +505,9 @@
         high = lax.ppermute(own, "wave", backward)
         coeffs = grid_step(
             jnp.concatenate([low, own, high], axis=0),
-            depart_row[k].reshape(stencil, grid_width),
-            depart_col[k].reshape(stencil, grid_width),
-            depart_weight[k].reshape(stencil, grid_width),
+            depart_row[k].reshape(1, stencil, 1, grid_width),
+            depart_col[k].reshape(1, stencil, 1, grid_width),
+            depart_weight[k].reshape(1, stencil, 1, grid_width),
             cos_rows, sin_rows, fc, fs, length1, coef_scale,
         )
         returned = lax.all_to_all(

time: 164 us -> 75.3 us (0.46)
  local copies, waits for them, and re-layouts: 37.8 us -> 1.91 us
  Pallas kernels: 33.8 us -> 64.3 us
  other arithmetic: 27 us -> 5.03 us
  starting transfers between devices: 21.7 us -> 0 us
  blocking collectives: 20.8 us -> 0 us
  matrix products: 17.9 us -> 0 us
    pallas_call x5 -> x3, Pallas kernels: 33.8 us -> 64.3 us  [the longest x1 45.3 us: fused(): pl.pallas_call(functools.partial(steps_kernel, steps, count, fields, bloc...]
    all_to_all x2 -> x0, blocking collectives: 20.8 us -> none  [the longest x1 10.8 us: per_device(): lax.all_to_all(fourier.astype(BF16), 'wave', split_axis=0, concat_axis=2,...]
    unnamed x2 -> x0, other arithmetic: 18.2 us -> none
    dot_general x4 -> x0, matrix products: 17.9 us -> none  [the longest x1 6.61 us: per_device(): jnp.einsum('sjn,skn->sjk', masked, masked, preferred_element_type=F32)]
    all_to_all x2 -> x0, starting transfers between devices: 12.2 us -> none  [the longest x1 6.35 us: per_device(): lax.all_to_all(fourier.astype(BF16), 'wave', split_axis=0, concat_axis=2,...]
    unnamed x19 -> x0, local copies, waits for them, and re-layouts: 10.2 us -> none
    ppermute x4 -> x0, starting transfers between devices: 9.47 us -> none  [the longest x2 6.91 us: per_device(): low = lax.ppermute(own, 'wave', forward)]
    all_to_all x8 -> x0, local copies, waits for them, and re-layouts: 8.71 us -> none  [the longest x6 7.32 us: per_device(): lax.all_to_all(coeffs.reshape(1, 2 * fields, orders_total), 'wave', split...]
  transfers between devices with their start and end apart: 6 -> 0, of which waited for: 0 -> 0; matrix products, arithmetic and copies ran while one was open for 12% -> 0% of each run, Pallas kernels for 2% -> 0%
where the time goes in v2:
time: 75.3 us; the launch traced here: 74.6 us
  Pallas kernels  64.3 us (85%)
  other arithmetic  5.03 us (7%)
  between operations  3.37 us (4%)
  local copies, waits for them, and re-layouts  1.91 us (3%)
    pallas_call x1, Pallas kernels, fused(): pl.pallas_call(functools.partial(steps_kernel, steps, count, fields, bloc...  45.3 us
    pallas_call x1, Pallas kernels, fused(): pl.pallas_call(functools.partial(forward_kernel, fields, slots, rows_j),...  10.8 us
    pallas_call x1, Pallas kernels, fused(): pl.pallas_call(functools.partial(inverse_kernel, fields, rows_j), grid=(g...  8.26 us
    sin x1, other arithmetic, phase_rows(): return (jnp.cos(angles), jnp.sin(angles))  4.24 us

profile of v2, /device:TPU:0, one launch (start us, length us, event | category | flops | bytes accessed | tf_op | source)
XLA Modules:
  0.0 74.6 jit_solution(1028831471131271609)
XLA Ops:
  0.7 1.3 %dynamic_slice.4.len_ref = s32[1]{0:T(128)} dynamic-slice(s32[8]{0:T(128)} %param.11, s32[]{:T(128)S(6)} %select_n.17), dynamic_slice_sizes={1} | dynamic-slice | bytes 12 | tf_op jit(solution)/shard_map/jit(dynamic_index_in_dim)/dynamic_slice | solution.py:451
  4.7 0.1 pad_add_fusion
  4.8 0.7 compare_convert_fusion
  5.5 0.6 reshape.35.active_ref
  6.0 4.2 %fusion.4 = (f32[40,1280]{1,0:T(8,128)}, f32[40,1280]{1,0:T(8,128)}) fusion(f32[]{:T(128)S(6)} %div.15, s32[]{:T(128)S(6)} %select_n.18, s32[1280]{0:T(1024)} %orders_ref.1, s32[40]{0:T(128)S(1)} %pad_add_fusion, pred[]{:T(512)S(6)} %lt.20), kind=kLoop, calls=%fused_computation.6 | loop fusion | flops 512000 | bytes 414889 | tf_op jit(solution)/shard_map/sin | solution.py:32
  10.3 10.8 %forward.1 = (f32[8,8,256]{2,1,0:T(8,128)}, f32[8,8,256]{2,1,0:T(8,128)}, bf16[1280,1280]{1,0:T(8,128)(2,1)}) custom-call(s32[1280]{0:T(1024)} %orders_ref.1, bf16[8,160,1280]{2,1,0:T(8,128)(2,1)} %bitcast.13, bf16[1280,1280]{1,0:T(8,128)(2,1)} %bitcast.14), custom_call_target="tpu_custom_call" | custom-call | tf_op jit(solution)/shard_map/forward/pallas_call | solution.py:363
  21.1 45.3 %steps.1.coef_ref = f32[10,8,128]{2,1,0:T(8,128)} custom-call(f32[8,8,256]{2,1,0:T(8,128)} %get-tuple-element.8.first_ref, f32[8,8,256]{2,1,0:T(8,128)} %get-tuple-element.9.gram_ref, f32[40,1280]{1,0:T(8,128)} %get-tuple-element.12.cos_ref, f32[40,1280]{1,0:T(8,128)} %get-tuple-element.11.sin_ref, f32[1,1280]{1,0:T(1,128)} %reshape.35.active_ref, ...), custom_call_target="tpu_custom_call" | custom-call | tf_op jit(solution)/shard_map/steps/pallas_call | solution.py:390
  66.3 8.3 %inverse.1 = bf16[8,160,1280]{2,1,0:T(8,128)(2,1)} custom-call(f32[10,8,128]{2,1,0:T(8,128)} %steps.1.coef_ref, bf16[1280,1280]{1,0:T(8,128)(2,1)} %get-tuple-element.10.masked_ref), custom_call_target="tpu_custom_call" | custom-call | tf_op jit(solution)/shard_map/inverse/pallas_call | solution.py:414
  (3 shorter events, 0.0 us)

commit v3 on v2

--- a/solution.py
+++ b/solution.py
@@ -172,6 +172,98 @@
     out_ref[...] = jnp.concatenate(rows, axis=0).astype(BF16)
 
 
+HALF = 256
+
+
+def fill_phases(orders, length, cos_ref, sin_ref):
+    limit = length.astype(F32)
+    inverse = 1.0 / jnp.full(orders.shape, limit)
+    turn = FULL_TURN / jnp.full(orders.shape, limit)
+    digit = lax.broadcasted_iota(jnp.int32, (RADIX, orders.shape[1]), 0)
+    for t in range(cos_ref.shape[0] // RADIX):
+        if t < 3:
+            step = digit * RADIX**t
+        else:
+            step = (digit + (t - 3) * RADIX) * BLOCK
+        product = step * orders
+        rest = product - jnp.floor(product.astype(F32) * inverse).astype(jnp.int32) * length
+        rest = jnp.where(rest < 0, rest + length, rest)
+        rest = jnp.where(rest >= length, rest - length, rest)
+        angle = rest.astype(F32) * turn
+        cos_ref[t * RADIX : (t + 1) * RADIX, :] = jnp.cos(angle)
+        sin_ref[t * RADIX : (t + 1) * RADIX, :] = jnp.sin(angle)
+
+
+def grid_rows(coeffs, cos_block, sin_block, fc_ref, fs_ref, length, scale):
+    fields = coeffs.shape[0] // 2
+    blocks = cos_block.shape[0]
+    reals, imags = [], []
+    for v in range(fields):
+        real = coeffs[2 * v : 2 * v + 1]
+        imag = coeffs[2 * v + 1 : 2 * v + 2]
+        reals.append((real * cos_block - imag * sin_block).astype(BF16))
+        imags.append((real * sin_block + imag * cos_block).astype(BF16))
+    dims = (((1,), (1,)), ((), ()))
+    out = lax.dot_general(
+        fc_ref[...], jnp.concatenate(reals, axis=0), dims, preferred_element_type=F32
+    ) + lax.dot_general(
+        fs_ref[...], jnp.concatenate(imags, axis=0), dims, preferred_element_type=F32
+    )
+    out = out.T
+    row = lax.broadcasted_iota(jnp.int32, out.shape, 0) % blocks
+    point = row * BLOCK + lax.broadcasted_iota(jnp.int32, out.shape, 1)
+    out = jnp.where(point < length, out * scale, 0.0)
+    parts = []
+    for v in range(fields):
+        rows = out[v * blocks : (v + 1) * blocks]
+        parts += [rows[:8, :HALF], rows[:8, HALF:], rows[8:12, :HALF], rows[8:12, HALF:]]
+    return jnp.concatenate(parts, axis=0)
+
+
+def pick_block(b, k, table, row_ref, col_ref, weight_ref, fields):
+    stencil = col_ref.shape[1]
+    lanes = pl.ds(pl.multiple_of(b * BLOCK, BLOCK), BLOCK)
+    iota = lax.broadcasted_iota(jnp.int32, (HALF, BLOCK), 0).astype(F32).astype(BF16)
+    sub = lax.broadcasted_iota(jnp.int32, (8, BLOCK), 0)
+    one = jnp.ones((), BF16)
+    zero = jnp.zeros((), BF16)
+    acc = [jnp.zeros((8, BLOCK), F32) for _ in range(fields)]
+    for p in range(stencil):
+        col = col_ref[k, p, :, lanes]
+        row = row_ref[k, p, :, lanes]
+        weight = weight_ref[k, p, :, lanes]
+        key = (col & (HALF - 1)).astype(F32).astype(BF16)
+        onehot = jnp.where(iota == key, one, zero)
+        found = jnp.dot(table, onehot, preferred_element_type=F32)
+        big = col // BLOCK
+        side = (col // HALF) & 1
+        which = (row + 1) * 24 + jnp.where(big < 8, side * 8 + big, 8 + side * 4 + big)
+        got = [jnp.zeros((8, BLOCK), F32) for _ in range(fields)]
+        for r in range(3):
+            for t in range(3):
+                hit = sub == which - (r * 24 + t * 8)
+                for v in range(fields):
+                    start = (r * fields + v) * 24 + t * 8
+                    got[v] = jnp.where(hit, found[start : start + 8], got[v])
+        for v in range(fields):
+            acc[v] = acc[v] + got[v] * weight
+    return [jnp.sum(a, axis=0, keepdims=True) for a in acc]
+
+
+def advance_fast(table, k, row_ref, col_ref, weight_ref, new_ref, length, fields, blocks, real_blocks):
+    new_ref[...] = jnp.zeros_like(new_ref)
+
+    def body(b, carry):
+        interp = pick_block(b, k, table, row_ref, col_ref, weight_ref, fields)
+        point = b * BLOCK + lax.broadcasted_iota(jnp.int32, (1, BLOCK), 1)
+        for v in range(fields):
+            value = interp[v] + 0.5 * interp[(v + 1) % fields] * jnp.tanh(interp[(v + 2) % fields])
+            new_ref[pl.ds(v * blocks + b, 1), :] = jnp.where(point < length, value, 0.0)
+        return carry
+
+    lax.fori_loop(0, real_blocks, body, 0)
+
+
 GROUP = 16
 MESH = pl.DeviceIdType.MESH
 
@@ -196,12 +288,15 @@
     state = spec_ref[...].reshape(fields * GROUP, spec_ref.shape[2])
     dims = (((1,), (1,)), ((), ()))
     size = GROUP * rows_j
-    prod = lax.dot_general(masked, state, dims, preferred_element_type=F32)
+    both = lax.dot_general(
+        masked, jnp.concatenate([state, masked], axis=0), dims, preferred_element_type=F32
+    )
+    prod = both[:, : fields * GROUP]
     row = lax.broadcasted_iota(jnp.int32, (size, fields * GROUP), 0) // rows_j
     col = lax.broadcasted_iota(jnp.int32, (size, fields * GROUP), 1) % GROUP
     prod = jnp.where(row == col, prod, 0.0)
     four_ref[g] = jnp.sum(prod.reshape(GROUP, rows_j, fields * GROUP), axis=0)
-    square = lax.dot_general(masked, masked, dims, preferred_element_type=F32)
+    square = both[:, fields * GROUP :]
     row = lax.broadcasted_iota(jnp.int32, (size, size), 0)
     col = lax.broadcasted_iota(jnp.int32, (size, size), 1)
     square = jnp.where(row // rows_j == col // rows_j, square, 0.0)
@@ -238,10 +333,9 @@
 
 def steps_kernel(
     steps, count, fields, blocks, real_blocks, slots,
-    first_ref, gram_ref, cos_ref, sin_ref, active_ref, row_ref, col_ref, weight_ref,
-    len_ref, grid_scale_ref, coef_scale_ref,
+    first_ref, gram_ref, orders_ref, row_ref, col_ref, weight_ref, len_ref, gauss_ref,
     out_ref,
-    fc_ref, fs_ref, ca_ref, sa_ref, spec_send, spec_recv, grid_send, grid_recv, tab_ref, coef_ref,
+    cos_ref, sin_ref, fc_ref, fs_ref, ca_ref, sa_ref, spec_send, spec_recv, grid_send, grid_recv, tab_ref, coef_ref,
     new_ref, spec_ssem, spec_rsem, grid_ssem, grid_rsem, halo_ssem, halo_rsem,
 ):
     tab_ref[...] = jnp.zeros_like(tab_ref)
@@ -265,10 +359,17 @@
         return copies
 
     copies = exchange(first_ref, spec_recv.at[0], spec_ssem.at[0], spec_rsem.at[0])
-    build_table(cos_ref, sin_ref, active_ref, fc_ref, fs_ref, ca_ref, sa_ref)
+    length = len_ref[me]
+    orders = orders_ref[...]
+    limit = jnp.minimum(orders.shape[1], (length - 1) // 2)
+    fill_phases(orders, length, cos_ref, sin_ref)
+    active = jnp.where(orders < limit, 1.0, 0.0)
+    build_table(cos_ref, sin_ref, active, fc_ref, fs_ref, ca_ref, sa_ref)
+    grid_scale = 1.0 / jnp.sqrt(jnp.full((1, BLOCK), limit.astype(F32)))
+    coef_scale = gauss_ref[0] * jnp.sqrt(2.0 / jnp.full(orders.shape, length.astype(F32)))
     cos_block = cos_ref[3 * RADIX : 3 * RADIX + blocks, :]
     sin_block = sin_ref[3 * RADIX : 3 * RADIX + blocks, :]
-    rows = fields // 2 * blocks
+    rows = fields // 2 * 24
     for k in range(steps):
         source = first_ref if k == 0 else spec_send.at[k - 1]
         for copy in copies:
@@ -276,8 +377,8 @@
         spec_recv[k, me] = source[me]
         for i in range(count):
             coef_ref[:, i * slots : (i + 1) * slots] = spec_recv[k, i, :, :slots]
-        own = synthesize(
-            coef_ref[...], cos_block, sin_block, fc_ref, fs_ref, len_ref[0], grid_scale_ref[0]
+        own = grid_rows(
+            coef_ref[...], cos_block, sin_block, fc_ref, fs_ref, length, grid_scale
         )
         tab_ref[k, 1] = own.astype(BF16)
         up = pltpu.make_async_remote_copy(
@@ -304,9 +405,9 @@
         def _():
             down.wait_recv()
 
-        table = tab_ref[k].reshape(3 * rows, BLOCK)
-        advance(
-            table, k, row_ref, col_ref, weight_ref, new_ref, len_ref[0],
+        table = tab_ref[k].reshape(3 * rows, HALF)
+        advance_fast(
+            table, k, row_ref, col_ref, weight_ref, new_ref, length,
             fields // 2, blocks, real_blocks,
         )
 
@@ -318,7 +419,7 @@
         def _():
             down.wait_send()
 
-        parts = analyse(new_ref, cos_block, sin_block, fc_ref, fs_ref, coef_scale_ref[0])
+        parts = analyse(new_ref, cos_block, sin_block, fc_ref, fs_ref, coef_scale)
         for v, part in enumerate(parts):
             coef_ref[v : v + 1, :] = part
         for i in range(count):
@@ -345,7 +446,7 @@
             out_ref[h, :, v * GROUP : (v + 1) * GROUP] = last[v, :, h * GROUP : (h + 1) * GROUP]
 
 
-def fused(spectrum, legendre, order_of_slot, length, gauss_weight, row, col, weight, count):
+def fused(spectrum, legendre, order_of_slot, reduced_length, gauss_weight, row, col, weight, count):
     slots, rows_j, degrees = legendre.shape
     fields = 2 * spectrum.shape[0]
     orders_total = order_of_slot.shape[0]
@@ -355,11 +456,6 @@
     groups = slots // GROUP
     size = GROUP * rows_j
     lanes = -(-slots // 128) * 128
-    order_limit = jnp.minimum(orders_total, (length - 1) // 2)
-    cos_rows, sin_rows = phase_rows(length, order_of_slot, blocks)
-    active = (order_of_slot < order_limit).astype(F32)[None, :]
-    grid_scale = (1.0 / jnp.sqrt(order_limit.astype(F32))).reshape(1)
-    coef_scale = (gauss_weight[0] * jnp.sqrt(2.0 / length.astype(F32))).reshape(1)
     send, gram, masked = pl.pallas_call(
         functools.partial(forward_kernel, fields, slots, rows_j),
         grid=(groups,),
@@ -390,13 +486,14 @@
     coeffs = pl.pallas_call(
         functools.partial(steps_kernel, steps, count, fields, blocks, real_blocks, slots),
         out_shape=jax.ShapeDtypeStruct((groups, rows_j, fields * GROUP), F32),
-        in_specs=[VMEM_SPEC] * 8 + [SMEM_SPEC] * 3,
+        in_specs=[VMEM_SPEC] * 6 + [SMEM_SPEC] * 2,
         out_specs=VMEM_SPEC,
-        scratch_shapes=[pltpu.VMEM((BLOCK, orders_total), BF16)] * 2
+        scratch_shapes=[pltpu.VMEM((3 * RADIX + blocks, orders_total), F32)] * 2
+        + [pltpu.VMEM((BLOCK, orders_total), BF16)] * 2
         + [pltpu.VMEM((RADIX * RADIX, orders_total), F32)] * 2
         + [pltpu.VMEM(shape, F32)] * 4
         + [
-            pltpu.VMEM((steps, 3, table_rows, BLOCK), BF16),
+            pltpu.VMEM((steps, 3, fields // 2 * 24, HALF), BF16),
             pltpu.VMEM((fields, orders_total), F32),
             pltpu.VMEM((table_rows, BLOCK), F32),
         ]
@@ -405,11 +502,11 @@
         compiler_params=pltpu.CompilerParams(collective_id=0, has_side_effects=True),
         name="steps",
     )(
-        send, gram, cos_rows, sin_rows, active,
+        send, gram, order_of_slot.reshape(1, orders_total),
         row.reshape(steps, stencil, 1, grid_width),
         col.reshape(steps, stencil, 1, grid_width),
         weight.reshape(steps, stencil, 1, grid_width),
-        length.reshape(1), grid_scale, coef_scale,
+        reduced_length, gauss_weight,
     )
     out = pl.pallas_call(
         functools.partial(inverse_kernel, fields, rows_j),
@@ -448,14 +545,14 @@
     real_blocks = grid_width // BLOCK
     blocks = padded_blocks(grid_width)
 
-    length = lax.dynamic_index_in_dim(reduced_length, own_index, keepdims=False)
-    fits = slot_count % GROUP == 0 and 2 * fields == 8
+    fits = slot_count % GROUP == 0 and 2 * fields == 8 and real_blocks <= 12
     if fits and legendre.shape[1] == 8 and count == 8:
         return fused(
-            spectrum, legendre, order_of_slot, length, gauss_weight,
+            spectrum, legendre, order_of_slot, reduced_length, gauss_weight,
             depart_row, depart_col, depart_weight, count,
         )
 
+    length = lax.dynamic_index_in_dim(reduced_length, own_index, keepdims=False)
     own_orders = lax.dynamic_slice_in_dim(order_of_slot, own_index * slot_count, slot_count)
     degrees = jnp.arange(legendre.shape[2], dtype=jnp.int32)
     masked = jnp.where(

time: 75.3 us -> 62.8 us (0.83)
  other arithmetic: 5.03 us -> 0 us
  Pallas kernels: 64.3 us -> 60.3 us
  between operations: 3.37 us -> 0.66 us
    sin x1 -> x0, other arithmetic: 4.24 us -> none  [phase_rows(): return (jnp.cos(angles), jnp.sin(angles))]
    pallas_call x1, Pallas kernels: 45.3 us -> 41.2 us  [fused(): pl.pallas_call(functools.partial(steps_kernel, steps, count, fields, bloc...]
    dynamic_slice x1 -> x0, local copies, waits for them, and re-layouts: 1.31 us -> none  [per_device(): length = lax.dynamic_index_in_dim(reduced_length, own_index, keepdims=False)]
    reshape x0 -> x1, local copies, waits for them, and re-layouts: none -> 1.3 us  [fused(): order_of_slot.reshape(1, orders_total)]
where the time goes in v3:
time: 62.8 us; the launch traced here: 62.2 us
  Pallas kernels  60.3 us (96%)
  local copies, waits for them, and re-layouts  1.3 us (2%)
  between operations  0.66 us (1%)
    pallas_call x1, Pallas kernels, fused(): pl.pallas_call(functools.partial(steps_kernel, steps, count, fields, bloc...  41.2 us
    pallas_call x1, Pallas kernels, fused(): pl.pallas_call(functools.partial(forward_kernel, fields, slots, rows_j),...  10.8 us
    pallas_call x1, Pallas kernels, fused(): pl.pallas_call(functools.partial(inverse_kernel, fields, rows_j), grid=(g...  8.26 us
    reshape x1, local copies, waits for them, and re-layouts, fused(): order_of_slot.reshape(1, orders_total)  1.3 us

profile of v3, /device:TPU:0, one launch (start us, length us, event | category | flops | bytes accessed | tf_op | source)
XLA Modules:
  0.0 62.2 jit_solution(12585425750241955774)
XLA Ops:
  0.7 1.3 %reshape.23.orders_ref = s32[1,1280]{1,0:T(1,128)} reshape(s32[1280]{0:T(1024)} %orders_ref.1) | data formatting | bytes 10240 | tf_op jit(solution)/shard_map/reshape | solution.py:505
  2.0 10.8 %forward.1 = (f32[8,8,256]{2,1,0:T(8,128)}, f32[8,8,256]{2,1,0:T(8,128)}, bf16[1280,1280]{1,0:T(8,128)(2,1)}) custom-call(s32[1280]{0:T(1024)} %orders_ref.1, bf16[8,160,1280]{2,1,0:T(8,128)(2,1)} %bitcast.8, bf16[1280,1280]{1,0:T(8,128)(2,1)} %bitcast.9), custom_call_target="tpu_custom_call" | custom-call | tf_op jit(solution)/shard_map/forward/pallas_call | solution.py:459
  12.7 41.2 %steps.1.coef_ref = f32[10,8,128]{2,1,0:T(8,128)} custom-call(f32[8,8,256]{2,1,0:T(8,128)} %get-tuple-element.8.first_ref, f32[8,8,256]{2,1,0:T(8,128)} %get-tuple-element.9.gram_ref, s32[1,1280]{1,0:T(1,128)} %reshape.23.orders_ref, s32[2,4,1,5632]{3,2,1,0:T(1,128)} %bitcast.10, s32[2,4,1,5632]{3,2,1,0:T(1,128)} %bitcast.11, f32[2,4,1,5632]{3,2,1,0:T(1,128)} %bitcast.12, ...), custom_call_target="tpu_custom_call" | custom-call | tf_op jit(solution)/shard_map/steps/pallas_call | solution.py:486
  54.0 8.3 %inverse.1 = bf16[8,160,1280]{2,1,0:T(8,128)(2,1)} custom-call(f32[10,8,128]{2,1,0:T(8,128)} %steps.1.coef_ref, bf16[1280,1280]{1,0:T(8,128)(2,1)} %get-tuple-element.10.masked_ref), custom_call_target="tpu_custom_call" | custom-call | tf_op jit(solution)/shard_map/inverse/pallas_call | solution.py:511

commit v4 on v3

--- a/solution.py
+++ b/solution.py
@@ -268,83 +268,115 @@
 MESH = pl.DeviceIdType.MESH
 
 
-def forward_kernel(
-    fields, slots, rows_j,
-    orders_ref, spec_ref, leg_ref, send_ref, gram_ref, masked_ref, four_ref, gram_raw_ref, vjs_ref,
-):
-    g = pl.program_id(0)
-    groups = pl.num_programs(0)
-    first = lax.axis_index("wave") * slots + g * GROUP
-    degree = lax.broadcasted_iota(jnp.int32, (rows_j, leg_ref.shape[1]), 1)
+def mask_group(g, first, orders_ref, leg_ref, rows_j):
+    degree = lax.broadcasted_iota(jnp.int32, (rows_j, leg_ref.shape[2]), 1)
     for pair in range(GROUP // 2):
+        rows = slice(2 * pair * rows_j, 2 * (pair + 1) * rows_j)
+        both = leg_ref[g, rows, :].astype(F32)
         parts = []
-        for s in (2 * pair, 2 * pair + 1):
-            rows = leg_ref[s * rows_j : (s + 1) * rows_j, :].astype(F32)
-            parts.append(jnp.where(degree >= orders_ref[first + s], rows, 0.0))
-        masked_ref[2 * pair * rows_j : 2 * (pair + 1) * rows_j, :] = jnp.concatenate(
-            parts, axis=0
-        ).astype(BF16)
-    masked = masked_ref[...]
-    state = spec_ref[...].reshape(fields * GROUP, spec_ref.shape[2])
-    dims = (((1,), (1,)), ((), ()))
+        for s in range(2):
+            keep = degree >= orders_ref[first + g * GROUP + 2 * pair + s]
+            parts.append(jnp.where(keep, both[s * rows_j : (s + 1) * rows_j], 0.0))
+        leg_ref[g, rows, :] = jnp.concatenate(parts, axis=0).astype(BF16)
+
+
+def forward_group(g, fields, rows_j, spec_ref, leg_ref, four_ref, square_ref):
+    masked = leg_ref[g]
+    state = spec_ref[g].reshape(fields * GROUP, spec_ref.shape[3])
+    both = lax.dot_general(
+        masked, jnp.concatenate([state, masked], axis=0), (((1,), (1,)), ((), ())),
+        preferred_element_type=F32,
+    )
     size = GROUP * rows_j
-    both = lax.dot_general(
-        masked, jnp.concatenate([state, masked], axis=0), dims, preferred_element_type=F32
-    )
-    prod = both[:, : fields * GROUP]
-    row = lax.broadcasted_iota(jnp.int32, (size, fields * GROUP), 0) // rows_j
-    col = lax.broadcasted_iota(jnp.int32, (size, fields * GROUP), 1) % GROUP
-    prod = jnp.where(row == col, prod, 0.0)
-    four_ref[g] = jnp.sum(prod.reshape(GROUP, rows_j, fields * GROUP), axis=0)
-    square = both[:, fields * GROUP :]
+    width = fields * GROUP
+    row = lax.broadcasted_iota(jnp.int32, (size, width), 0) // rows_j
+    col = lax.broadcasted_iota(jnp.int32, (size, width), 1) % GROUP
+    prod = jnp.where(row == col, both[:, :width], 0.0)
+    four_ref[g] = jnp.sum(prod.reshape(GROUP, rows_j, width), axis=0)
     row = lax.broadcasted_iota(jnp.int32, (size, size), 0)
     col = lax.broadcasted_iota(jnp.int32, (size, size), 1)
-    square = jnp.where(row // rows_j == col // rows_j, square, 0.0)
-    diag = jnp.sum(square.reshape(GROUP, rows_j, size), axis=0)
+    square = jnp.where(row // rows_j == col // rows_j, both[:, width:], 0.0)
+    square_ref[g] = jnp.sum(square.reshape(GROUP, rows_j, size), axis=0)
+
+
+def gram_of(square_ref, gram_ref, rows_j):
+    groups, _, size = square_ref.shape
+    row = lax.broadcasted_iota(jnp.int32, (size, size), 0)
+    col = lax.broadcasted_iota(jnp.int32, (size, size), 1)
     swap = (row // rows_j == col % GROUP) & (row % rows_j == col // GROUP)
-    gram_raw_ref[g] = jnp.dot(
-        diag, jnp.where(swap, 1.0, 0.0), preferred_element_type=F32, precision="highest"
-    )
-
-    @pl.when(g == groups - 1)
-    def _():
-        vjs_ref[...] = jnp.zeros_like(vjs_ref)
-        gram_ref[...] = jnp.zeros_like(gram_ref)
-        for h in range(slots // GROUP):
-            lanes = slice(h * GROUP, (h + 1) * GROUP)
-            for v in range(fields):
-                vjs_ref[v, :, lanes] = four_ref[h, :, v * GROUP : (v + 1) * GROUP]
-            for j in range(rows_j):
-                gram_ref[j, :, lanes] = gram_raw_ref[h, :, j * GROUP : (j + 1) * GROUP]
-        send_ref[...] = jnp.swapaxes(vjs_ref[...], 0, 1)
-
-
-def inverse_kernel(fields, rows_j, coef_ref, masked_ref, out_ref):
+    turned = jnp.dot(
+        square_ref[...].reshape(groups * rows_j, size), jnp.where(swap, 1.0, 0.0),
+        preferred_element_type=F32, precision="highest",
+    )
+    gram_ref[...] = jnp.zeros_like(gram_ref)
+    for h in range(groups):
+        rows = turned[h * rows_j : (h + 1) * rows_j]
+        for j in range(rows_j):
+            gram_ref[j, :, h * GROUP : (h + 1) * GROUP] = rows[:, j * GROUP : (j + 1) * GROUP]
+
+
+def inverse_group(g, fields, rows_j, coef_ref, leg_ref, out_ref):
     size = GROUP * rows_j
     row = lax.broadcasted_iota(jnp.int32, (size, fields * GROUP), 0) // rows_j
     col = lax.broadcasted_iota(jnp.int32, (size, fields * GROUP), 1) % GROUP
-    tiled = jnp.concatenate([coef_ref[0]] * GROUP, axis=0)
-    spread = jnp.where(row == col, tiled, 0.0).astype(BF16)
-    out = lax.dot_general(
-        spread, masked_ref[...], (((0,), (0,)), ((), ())), preferred_element_type=F32
-    )
-    out_ref[...] = out.astype(BF16).reshape(out_ref.shape)
+    tiled = jnp.concatenate([coef_ref[g]] * GROUP, axis=0)
+    spread = jnp.where(row == col, tiled, 0.0).T.astype(BF16)
+    out = jnp.dot(spread, leg_ref[g], preferred_element_type=F32)
+    out_ref[g] = out.astype(BF16).reshape(out_ref.shape[1:])
 
 
 def steps_kernel(
     steps, count, fields, blocks, real_blocks, slots,
-    first_ref, gram_ref, orders_ref, row_ref, col_ref, weight_ref, len_ref, gauss_ref,
-    out_ref,
+    spec_hbm, leg_hbm, orders_ref, row_ref, col_ref, weight_ref, order_ref, len_ref, gauss_ref,
+    out_hbm,
+    spec_ref, leg_ref, four_ref, square_ref, vjs_ref, first_ref, gram_ref, load_sem, out_sem,
     cos_ref, sin_ref, fc_ref, fs_ref, ca_ref, sa_ref, spec_send, spec_recv, grid_send, grid_recv, tab_ref, coef_ref,
     new_ref, spec_ssem, spec_rsem, grid_ssem, grid_rsem, halo_ssem, halo_rsem,
 ):
+    rows_j = leg_ref.shape[1] // GROUP
+    groups = slots // GROUP
+
+    def loads(g):
+        slot_rows = pl.ds(pl.multiple_of(g * GROUP, GROUP), GROUP)
+        return (
+            pltpu.make_async_copy(leg_hbm.at[g], leg_ref.at[g], load_sem.at[0, g]),
+            pltpu.make_async_copy(spec_hbm.at[:, slot_rows, :], spec_ref.at[g], load_sem.at[1, g]),
+        )
+
+    def store(g):
+        slot_rows = pl.ds(pl.multiple_of(g * GROUP, GROUP), GROUP)
+        return pltpu.make_async_copy(spec_ref.at[g], out_hbm.at[:, slot_rows, :], out_sem.at[g])
+
+    for g in range(groups):
+        for copy in loads(g):
+            copy.start()
     tab_ref[...] = jnp.zeros_like(tab_ref)
+    vjs_ref[...] = jnp.zeros_like(vjs_ref)
     grid_send[...] = jnp.zeros_like(grid_send)
     me = lax.axis_index("wave")
     peers = [lax.rem(me + d, count) for d in range(1, count)]
     barrier = pltpu.get_barrier_semaphore()
     for peer in peers:
         pl.semaphore_signal(barrier, inc=1, device_id={"wave": peer}, device_id_type=MESH)
+    length = len_ref[me]
+    orders = orders_ref[...]
+    limit = jnp.minimum(orders.shape[1], (length - 1) // 2)
+    fill_phases(orders, length, cos_ref, sin_ref)
+
+    def forward(g, carry):
+        for copy in loads(g):
+            copy.wait()
+        mask_group(g, me * slots, order_ref, leg_ref, rows_j)
+        forward_group(g, fields, rows_j, spec_ref, leg_ref, four_ref, square_ref)
+        return carry
+
+    lax.fori_loop(0, groups, forward, 0)
+    for h in range(groups):
+        for v in range(fields):
+            vjs_ref[v, :, h * GROUP : (h + 1) * GROUP] = four_ref[
+                h, :, v * GROUP : (v + 1) * GROUP
+            ]
+    first_ref[...] = jnp.swapaxes(vjs_ref[...], 0, 1)
     pl.semaphore_wait(barrier, count - 1)
 
     def exchange(send, recv, ssem, rsem):
@@ -359,10 +391,7 @@
         return copies
 
     copies = exchange(first_ref, spec_recv.at[0], spec_ssem.at[0], spec_rsem.at[0])
-    length = len_ref[me]
-    orders = orders_ref[...]
-    limit = jnp.minimum(orders.shape[1], (length - 1) // 2)
-    fill_phases(orders, length, cos_ref, sin_ref)
+    gram_of(square_ref, gram_ref, rows_j)
     active = jnp.where(orders < limit, 1.0, 0.0)
     build_table(cos_ref, sin_ref, active, fc_ref, fs_ref, ca_ref, sa_ref)
     grid_scale = 1.0 / jnp.sqrt(jnp.full((1, BLOCK), limit.astype(F32)))
@@ -443,7 +472,16 @@
     last = jnp.swapaxes(grid_recv[steps - 1], 0, 1)
     for h in range(slots // GROUP):
         for v in range(fields):
-            out_ref[h, :, v * GROUP : (v + 1) * GROUP] = last[v, :, h * GROUP : (h + 1) * GROUP]
+            four_ref[h, :, v * GROUP : (v + 1) * GROUP] = last[v, :, h * GROUP : (h + 1) * GROUP]
+
+    def inverse(g, carry):
+        inverse_group(g, fields, rows_j, four_ref, leg_ref, spec_ref)
+        store(g).start()
+        return carry
+
+    lax.fori_loop(0, groups, inverse, 0)
+    for g in range(groups):
+        store(g).wait()
 
 
 def fused(spectrum, legendre, order_of_slot, reduced_length, gauss_weight, row, col, weight, count):
@@ -456,39 +494,25 @@
     groups = slots // GROUP
     size = GROUP * rows_j
     lanes = -(-slots // 128) * 128
-    send, gram, masked = pl.pallas_call(
-        functools.partial(forward_kernel, fields, slots, rows_j),
-        grid=(groups,),
-        out_shape=[
-            jax.ShapeDtypeStruct((rows_j, fields, lanes), F32),
-            jax.ShapeDtypeStruct((rows_j, rows_j, lanes), F32),
-            jax.ShapeDtypeStruct((slots * rows_j, degrees), BF16),
-        ],
-        in_specs=[
-            SMEM_SPEC,
-            pl.BlockSpec((fields, GROUP, degrees), lambda g: (0, g, 0)),
-            pl.BlockSpec((size, degrees), lambda g: (g, 0)),
-        ],
-        out_specs=[
-            pl.BlockSpec((rows_j, fields, lanes), lambda g: (0, 0, 0)),
-            pl.BlockSpec((rows_j, rows_j, lanes), lambda g: (0, 0, 0)),
-            pl.BlockSpec((size, degrees), lambda g: (g, 0)),
-        ],
+    shape = (steps, count, fields, lanes)
+    table_rows = fields // 2 * blocks
+    out = pl.pallas_call(
+        functools.partial(steps_kernel, steps, count, fields, blocks, real_blocks, slots),
+        out_shape=jax.ShapeDtypeStruct((fields, slots, degrees), BF16),
+        in_specs=[pl.BlockSpec(memory_space=pl.ANY)] * 2 + [VMEM_SPEC] * 4 + [SMEM_SPEC] * 3,
+        out_specs=pl.BlockSpec(memory_space=pl.ANY),
         scratch_shapes=[
+            pltpu.VMEM((groups, fields, GROUP, degrees), BF16),
+            pltpu.VMEM((groups, size, degrees), BF16),
             pltpu.VMEM((groups, rows_j, fields * GROUP), F32),
             pltpu.VMEM((groups, rows_j, size), F32),
             pltpu.VMEM((fields, rows_j, lanes), F32),
-        ],
-        name="forward",
-    )(order_of_slot, spectrum.reshape(fields, slots, degrees), legendre.reshape(slots * rows_j, degrees))
-    shape = (steps, count, fields, lanes)
-    table_rows = fields // 2 * blocks
-    coeffs = pl.pallas_call(
-        functools.partial(steps_kernel, steps, count, fields, blocks, real_blocks, slots),
-        out_shape=jax.ShapeDtypeStruct((groups, rows_j, fields * GROUP), F32),
-        in_specs=[VMEM_SPEC] * 6 + [SMEM_SPEC] * 2,
-        out_specs=VMEM_SPEC,
-        scratch_shapes=[pltpu.VMEM((3 * RADIX + blocks, orders_total), F32)] * 2
+            pltpu.VMEM((rows_j, fields, lanes), F32),
+            pltpu.VMEM((rows_j, rows_j, lanes), F32),
+            pltpu.SemaphoreType.DMA((2, groups)),
+            pltpu.SemaphoreType.DMA((groups,)),
+        ]
+        + [pltpu.VMEM((3 * RADIX + blocks, orders_total), F32)] * 2
         + [pltpu.VMEM((BLOCK, orders_total), BF16)] * 2
         + [pltpu.VMEM((RADIX * RADIX, orders_total), F32)] * 2
         + [pltpu.VMEM(shape, F32)] * 4
@@ -502,23 +526,14 @@
         compiler_params=pltpu.CompilerParams(collective_id=0, has_side_effects=True),
         name="steps",
     )(
-        send, gram, order_of_slot.reshape(1, orders_total),
+        spectrum.reshape(fields, slots, degrees),
+        legendre.reshape(groups, size, degrees),
+        order_of_slot.reshape(1, orders_total),
         row.reshape(steps, stencil, 1, grid_width),
         col.reshape(steps, stencil, 1, grid_width),
         weight.reshape(steps, stencil, 1, grid_width),
-        reduced_length, gauss_weight,
-    )
-    out = pl.pallas_call(
-        functools.partial(inverse_kernel, fields, rows_j),
-        grid=(groups,),
-        out_shape=jax.ShapeDtypeStruct((fields, slots, degrees), BF16),
-        in_specs=[
-            pl.BlockSpec((1, rows_j, fields * GROUP), lambda g: (g, 0, 0)),
-            pl.BlockSpec((size, degrees), lambda g: (g, 0)),
-        ],
-        out_specs=pl.BlockSpec((fields, GROUP, degrees), lambda g: (0, g, 0)),
-        name="inverse",
-    )(coeffs, masked)
+        order_of_slot, reduced_length, gauss_weight,
+    )
     return out.reshape(spectrum.shape)
 
 

time: 62.8 us -> 54.3 us (0.86)
  Pallas kernels: 60.3 us -> 48.3 us
  local copies, waits for them, and re-layouts: 1.3 us -> 5.14 us
    pallas_call x2 -> x0, Pallas kernels: 19.1 us -> none  [the longest x1 10.8 us: fused(): pl.pallas_call(functools.partial(forward_kernel, fields, slots, rows_j),...]
    pallas_call x1, Pallas kernels: 41.2 us -> 48.3 us  [fused(): pl.pallas_call(functools.partial(steps_kernel, steps, count, fields, bloc...]
    unnamed x0 -> x1, local copies, waits for them, and re-layouts: none -> 3.84 us
where the time goes in v4:
time: 54.3 us; the launch traced here: 54.1 us
  Pallas kernels  48.3 us (89%)
  local copies, waits for them, and re-layouts  5.14 us (9%)
  between operations  0.66 us (1%)
    pallas_call x1, Pallas kernels, fused(): pl.pallas_call(functools.partial(steps_kernel, steps, count, fields, bloc...  48.3 us
    unnamed x1, local copies, waits for them, and re-layouts  3.84 us
    reshape x1, local copies, waits for them, and re-layouts, fused(): order_of_slot.reshape(1, orders_total)  1.3 us

profile of v4, /device:TPU:0, one launch (start us, length us, event | category | flops | bytes accessed | tf_op | source)
XLA Modules:
  0.0 54.1 jit_solution(8869975685129094071)
XLA Ops:
  0.7 1.3 %reshape.23.orders_ref = s32[1,1280]{1,0:T(1,128)} reshape(s32[1280]{0:T(1024)} %order_ref.1) | data formatting | bytes 10240 | tf_op jit(solution)/shard_map/reshape | solution.py:531
  1.9 48.3 %steps.1 = bf16[8,160,1280]{2,1,0:T(8,128)(2,1)} custom-call(bf16[8,160,1280]{2,1,0:T(8,128)(2,1)} %bitcast.9, bf16[10,128,1280]{2,1,0:T(8,128)(2,1)} %bitcast.10, s32[1,1280]{1,0:T(1,128)} %reshape.23.orders_ref, s32[2,4,1,5632]{3,2,1,0:T(1,128)} %bitcast.11, s32[2,4,1,5632]{3,2,1,0:T(1,128)} %bitcast.12, f32[2,4,1,5632]{3,2,1,0:T(1,128)} %bitcast.13, ...), custom_call_target="tpu_custom_call" | custom-call | tf_op jit(solution)/shard_map/steps/pallas_call | solution.py:499
  50.3 3.8 %copy.12 = bf16[4,1,2,160,1280]{4,3,2,1,0:T(8,128)(2,1)} copy(bf16[4,1,2,160,1280]{4,3,2,1,0:T(8,128)(2,1)} %bitcast.8) | data formatting | bytes 6553600

commit v5 on v4

--- a/solution.py
+++ b/solution.py
@@ -370,7 +370,7 @@
         forward_group(g, fields, rows_j, spec_ref, leg_ref, four_ref, square_ref)
         return carry
 
-    lax.fori_loop(0, groups, forward, 0)
+    lax.fori_loop(0, groups, forward, 0, unroll=2)
     for h in range(groups):
         for v in range(fields):
             vjs_ref[v, :, h * GROUP : (h + 1) * GROUP] = four_ref[
@@ -479,7 +479,7 @@
         store(g).start()
         return carry
 
-    lax.fori_loop(0, groups, inverse, 0)
+    lax.fori_loop(0, groups, inverse, 0, unroll=2)
     for g in range(groups):
         store(g).wait()
 

time: 54.3 us -> 53.9 us (level)
  no operation moved by 1% of the time
where the time goes in v5:
time: 53.9 us; the launch traced here: 53.7 us
  Pallas kernels  47.9 us (89%)
  local copies, waits for them, and re-layouts  5.14 us (10%)
  between operations  0.66 us (1%)
    pallas_call x1, Pallas kernels, fused(): pl.pallas_call(functools.partial(steps_kernel, steps, count, fields, bloc...  47.9 us
    unnamed x1, local copies, waits for them, and re-layouts  3.84 us
    reshape x1, local copies, waits for them, and re-layouts, fused(): order_of_slot.reshape(1, orders_total)  1.3 us

profile of v5, /device:TPU:0, one launch (start us, length us, event | category | flops | bytes accessed | tf_op | source)
XLA Modules:
  0.0 53.7 jit_solution(5951783866335498347)
XLA Ops:
  0.7 1.3 %reshape.23.orders_ref = s32[1,1280]{1,0:T(1,128)} reshape(s32[1280]{0:T(1024)} %order_ref.1) | data formatting | bytes 10240 | tf_op jit(solution)/shard_map/reshape | solution.py:531
  1.9 47.9 %steps.1 = bf16[8,160,1280]{2,1,0:T(8,128)(2,1)} custom-call(bf16[8,160,1280]{2,1,0:T(8,128)(2,1)} %bitcast.9, bf16[10,128,1280]{2,1,0:T(8,128)(2,1)} %bitcast.10, s32[1,1280]{1,0:T(1,128)} %reshape.23.orders_ref, s32[2,4,1,5632]{3,2,1,0:T(1,128)} %bitcast.11, s32[2,4,1,5632]{3,2,1,0:T(1,128)} %bitcast.12, f32[2,4,1,5632]{3,2,1,0:T(1,128)} %bitcast.13, ...), custom_call_target="tpu_custom_call" | custom-call | tf_op jit(solution)/shard_map/steps/pallas_call | solution.py:499
  49.8 3.8 %copy.12 = bf16[4,1,2,160,1280]{4,3,2,1,0:T(8,128)(2,1)} copy(bf16[4,1,2,160,1280]{4,3,2,1,0:T(8,128)(2,1)} %bitcast.8) | data formatting | bytes 6553600
